TPU v7x, 256 devices: a whole 4x4x8 slice. The times are simulated.
256 devices in a mesh: lon: 16 (over x_hi, y, core), rad: 16 (over z, x_lo).
Axes of the slice: x: 4 (x_hi: 2, x_lo: 2; x = x_hi * 2 + x_lo), y: 4, z: 8, core: 2. Of those that a mesh axis runs over, the one named last changes fastest.
Arguments:
- state: float32 [5, 128, 48, 2048], P(None, 'rad', None, 'lon'), may hold values from -6 to 6
- outer_rows: float32 [5, 128, 4, 2048], P(None, 'rad', None, 'lon'), may hold values from -6 to 6
- kappa: float32 [128], P('rad'), may hold values from 5e-05 to 0.0005
Outputs:
- increment: float32 [5, 128, 48, 2048], P(None, 'rad', None, 'lon')
All inputs are finite; a program needn't handle non-finite values.
Results may differ from a plain program's by a relative error of at most 0.00002.
Values sent between devices are 32-bit elements; how exact they have to be, the bound alone decides.
A program may use at most 128 MiB of HBM per device.

v0:
```python
import math

import jax
import jax.numpy as jnp
from jax import lax
from jax.sharding import PartitionSpec as P

first_coeffs = (0.8, -0.2, 4.0 / 105.0, -1.0 / 280.0)
second_coeffs = (-205.0 / 72.0, 1.6, -0.2, 8.0 / 315.0, -1.0 / 560.0)
time_step = 0.002
gamma_less_one = 0.4
radial_ratio = 3.0


def with_halo(block, sides, width, periodic):
    for axis, dim in sides:
        count = lax.axis_size(axis)
        forward = [(i, i + 1) for i in range(count - 1)]
        if periodic:
            forward.append((count - 1, 0))
        backward = [(target, source) for source, target in forward]
        low = lax.ppermute(
            lax.slice_in_dim(block, block.shape[dim] - width, None, axis=dim), axis, forward
        )
        high = lax.ppermute(lax.slice_in_dim(block, 0, width, axis=dim), axis, backward)
        block = jnp.concatenate([low, block, high], axis=dim)
    return block


def passed_along(array, axis, by):
    peers = lax.axis_size(axis)
    return lax.ppermute(array, axis, [(i, (i + by) % peers) for i in range(peers)])


def window(padded, offset, length, axis):
    return lax.slice_in_dim(padded, offset, offset + length, axis=axis)


def first_derivative(padded, length, axis):
    total = first_coeffs[0] * (window(padded, 5, length, axis) - window(padded, 3, length, axis))
    for reach in range(2, 5):
        total = total + first_coeffs[reach - 1] * (
            window(padded, 4 + reach, length, axis) - window(padded, 4 - reach, length, axis)
        )
    return total


def second_derivative(padded, length, axis):
    total = second_coeffs[0] * window(padded, 4, length, axis)
    for reach in range(1, 5):
        total = total + second_coeffs[reach] * (
            window(padded, 4 + reach, length, axis) + window(padded, 4 - reach, length, axis)
        )
    return total


def geometry(rows, nlon):
    index = jnp.arange(rows, dtype=jnp.float32)
    spacing = 2.0 * math.pi / nlon
    theta = (index + 0.5) * spacing
    metric = 1.0 / jnp.sin(theta)
    return (metric[:, None], (jnp.cos(theta) * metric)[:, None])


def tendency(center, pad_lon, pad_row, pad_level, kappa_col, metric, curvature):
    levels, rows, width = (center.shape[1], center.shape[2], center.shape[3])
    slope_lon = metric * first_derivative(pad_lon, width, 3)
    slope_row = first_derivative(pad_row, rows, 2)
    slope_level = radial_ratio * first_derivative(pad_level, levels, 1)
    wind_lon = center[1]
    wind_row = center[2]
    wind_level = center[3]
    temper = center[4]
    carried = wind_lon * slope_lon + wind_row * slope_row + wind_level * slope_level
    spread = slope_lon[1] + slope_row[2] + slope_level[3] + curvature * wind_row
    laplace = (
        metric * metric * second_derivative(pad_lon[4], width, 2)
        + second_derivative(pad_row[4], rows, 1)
        + radial_ratio * radial_ratio * second_derivative(pad_level[4], levels, 0)
    )
    return jnp.stack(
        [
            -carried[0] - spread,
            -carried[1] - temper * slope_lon[0] - slope_lon[4],
            -carried[2] - temper * slope_row[0] - slope_row[4],
            -carried[3] - temper * slope_level[0] - slope_level[4],
            -carried[4] - gamma_less_one * temper * spread + kappa_col * laplace,
        ]
    )


def neighbours(center, outer_rows):
    flip_signs = jnp.array([1.0, -1.0, -1.0, 1.0, 1.0], dtype=jnp.float32).reshape(5, 1, 1, 1)
    pad_lon = with_halo(center, (("lon", 3),), 4, True)
    across = passed_along(center[:, :, :4, :], "lon", lax.axis_size("lon") // 2)
    pad_row = jnp.concatenate([across[:, :, ::-1, :] * flip_signs, center, outer_rows], axis=2)
    return (pad_lon, pad_row)


def on_device(state, outer_rows, kappa):
    levels = state.shape[1]
    metric, curvature = geometry(state.shape[2], state.shape[3] * lax.axis_size("lon"))
    kappa_col = kappa.reshape(levels, 1, 1)
    current = state
    rates = []
    for turn in range(2):
        pad_lon, pad_row = neighbours(current, outer_rows)
        pad_level = with_halo(current, (("rad", 1),), 4, False)
        rate = tendency(current, pad_lon, pad_row, pad_level, kappa_col, metric, curvature)
        rates.append(rate)
        current = current + time_step * rate
    first, second = (rates[0], rates[1])
    return 0.5 * time_step * (first + second)


def solution(mesh):
    placed = (P(None, "rad", None, "lon"), P(None, "rad", None, "lon"), P("rad"))
    return jax.shard_map(
        on_device,
        mesh=mesh,
        in_specs=placed,
        out_specs=P(None, "rad", None, "lon"),
        check_vma=False,
    )
```

profile of v0, /device:TPU:98, one launch (start us, length us, event | category | flops | bytes accessed | tf_op | source)
XLA Modules:
  0.0 206.2 jit_solution(12242215830273112767)
XLA Ops:
  2.2 5.0 %collective-permute-start.4 = (f32[5,4,48,128]{3,2,1,0:T(8,128)}, f32[5,4,48,128]{3,2,1,0:T(8,128)}, u32[]{:S(2)}, u32[]{:S(2)}) collective-permute-start(f32[5,4,48,128]{3,2,1,0:T(8,128)} %get-tuple-element.46), channel_id=1, source_target_pairs={{0,1},{1,2},{2,3},{3,4},{4,5},{5,6},{6,7},{7,8},{8,9},{9,10},{10,1... | collective-permute-start | bytes 1474568 | tf_op jit(solution)/shard_map/ppermute | solution.py:22
  11.5 5.3 %collective-permute-start = (f32[5,8,48,4]{2,1,3,0:T(8,128)S(1)}, f32[5,8,48,4]{2,1,3,0:T(8,128)S(1)}, u32[]{:S(2)}, u32[]{:S(2)}) collective-permute-start(f32[5,8,48,4]{2,1,3,0:T(8,128)S(1)} %get-tuple-element.24), channel_id=1, source_target_pairs={{16,0},{32,16},{48,32},{64,48},{80,64},{96,80},{112,96},{128,112},... | collective-permute-start | bytes 92168 | tf_op jit(solution)/shard_map/ppermute | solution.py:25
  25.8 8.0 %collective-permute-done.1 = f32[5,8,48,4]{2,1,3,0:T(8,128)S(1)} collective-permute-done((f32[5,8,48,4]{2,1,3,0:T(8,128)S(1)}, f32[5,8,48,4]{2,1,3,0:T(8,128)S(1)}, u32[]{:S(2)}, u32[]{:S(2)}) %collective-permute-start.1) | collective-permute-done | bytes 30752 | tf_op jit(solution)/shard_map/ppermute | solution.py:22
  47.6 3.2 %copy.216 = f32[5,8,48,128]{2,1,3,0:T(8,128)} copy(f32[5,8,48,128]{3,2,1,0:T(8,128)} %get-tuple-element.41) | data formatting | bytes 1966080
  50.8 3.0 %copy.217 = f32[5,8,48,128]{2,1,3,0:T(8,128)} copy(f32[5,8,48,128]{3,2,1,0:T(8,128)} %get-tuple-element.37) | data formatting | bytes 1966080
  53.8 3.1 %copy.214 = f32[5,8,48,128]{2,1,3,0:T(8,128)} copy(f32[5,8,48,128]{3,2,1,0:T(8,128)} %get-tuple-element.42) | data formatting | bytes 1966080
  56.9 3.0 %copy.215 = f32[5,8,48,128]{2,1,3,0:T(8,128)} copy(f32[5,8,48,128]{3,2,1,0:T(8,128)} %get-tuple-element.38) | data formatting | bytes 1966080
  59.9 3.0 %copy.212 = f32[5,8,48,128]{2,1,3,0:T(8,128)} copy(f32[5,8,48,128]{3,2,1,0:T(8,128)} %get-tuple-element.43) | data formatting | bytes 1966080
  63.0 3.1 %copy.213 = f32[5,8,48,128]{2,1,3,0:T(8,128)} copy(f32[5,8,48,128]{3,2,1,0:T(8,128)} %get-tuple-element.39) | data formatting | bytes 1966080
  66.0 3.1 %copy.210 = f32[5,8,48,128]{2,1,3,0:T(8,128)} copy(f32[5,8,48,128]{3,2,1,0:T(8,128)} %get-tuple-element.40) | data formatting | bytes 1966080
  69.1 3.0 %copy.211 = f32[5,8,48,128]{2,1,3,0:T(8,128)} copy(f32[5,8,48,128]{3,2,1,0:T(8,128)} %get-tuple-element.36) | data formatting | bytes 1966080
  72.2 10.6 %broadcast_multiply_fusion.1 = (f32[5,8,48,128]{2,1,3,0:T(8,128)}, f32[5,8,48,128]{2,1,3,0:T(8,128)}) fusion(f32[5,8,48,128]{2,1,3,0:T(8,128)} %copy.216, f32[5,8,48,128]{2,1,3,0:T(8,128)} %copy.217, f32[5,8,48,128]{2,1,3,0:T(8,128)} %copy.214, f32[5,8,48,128]{2,1,3,0:T(8,128)} %copy.215, f32[5,8,48,128]{2,1,3,0:T(8,128)} %copy.212, ...), kind=kLoop, calls=%fused_computation.147 | loop fusion | flops 2949120 | bytes 9830400 | tf_op jit(solution)/shard_map/mul | solution.py:69
  82.8 15.5 %multiply_add_fusion.2 = (f32[5,8,48,128]{2,1,3,0:T(8,128)S(1)}, f32[5,8,48,128]{2,1,3,0:T(8,128)S(1)}, f32[5,8,48,128]{2,1,3,0:T(8,128)}) fusion(f32[5,8,48,128]{2,1,3,0:T(8,128)} %get-tuple-element.13, f32[8,48,128]{1,0,2:T(8,128)} %get-tuple-element.27, f32[8,48,128]{1,0,2:T(8,128)} %get-tuple-element.26, f32[8,48,128]{1,0,2:T(8,128)} %copy.165, ...), kind=kLoop, calls=%fused_computation.142 | loop fusion | flops 10813440 | bytes 5730496 | tf_op jit(solution)/shard_map/add | solution.py:74
  98.3 2.5 %fusion.168 = f32[5,8,48,128]{2,1,3,0:T(8,128)} fusion(f32[5,8,48,128]{2,1,3,0:T(8,128)S(1)} %get-tuple-element.14, f32[5,8,48,128]{2,1,3,0:T(8,128)S(1)} %copy.167, f32[48]{0:T(128)S(1)} %get-tuple-element.48, f32[5,8,48,128]{2,1,3,0:T(8,128)S(1)} %copy-done.9, f32[5,8,48,128]{2,1,3,0:T(8,128)} %get-tuple-element.16, ...), kind=kLoop, calls=%fused_computation.295 | loop fusion | flops 294911 | bytes 1507520
  118.5 6.5 %fusion.141 = f32[5,8,48,128]{2,1,3,0:T(8,128)} fusion(f32[5,8,48,128]{2,1,3,0:T(8,128)} %fusion.161, f32[8,56,128]{1,0,2:T(8,128)S(1)} %get-tuple-element.10, f32[8,48,136]{1,0,2:T(8,128)} %fusion.78, f32[5,8,48,128]{2,1,3,0:T(8,128)} %copy-done.7, f32[1,8,48,128]{2,1,3,0:T(8,128)} %copy.224, f32[1,8,48,128]{2,1,3,0:T(8,128)} %copy.225, ...), kind=kLoop, calls=%fused_computation.245 | loop fusion | flops 2605056 | bytes 13697440 | tf_op jit(solution)/shard_map/stack | solution.py:81
  124.9 2.8 %multiply_add_fusion.1 = f32[5,8,48,128]{2,1,3,0:T(8,128)S(1)} fusion(f32[5,8,48,128]{2,1,3,0:T(8,128)} %copy-done, f32[5,8,48,128]{2,1,3,0:T(8,128)} %fusion.141), kind=kLoop, calls=%fused_computation.141 | loop fusion | flops 491520 | bytes 2949120 | tf_op jit(solution)/shard_map/add | solution.py:111
  129.8 5.3 %collective-permute-start.5 = (f32[5,8,48,4]{2,1,3,0:T(8,128)S(1)}, f32[5,8,48,4]{2,1,3,0:T(8,128)S(1)}, u32[]{:S(2)}, u32[]{:S(2)}) collective-permute-start(f32[5,8,48,4]{2,1,3,0:T(8,128)S(1)} %get-tuple-element.17), channel_id=1, source_target_pairs={{16,0},{32,16},{48,32},{64,48},{80,64},{96,80},{112,96},{128,112},... | collective-permute-start | bytes 92168 | tf_op jit(solution)/shard_map/ppermute | solution.py:25
  138.8 4.3 %collective-permute-start.9 = (f32[5,4,48,128]{3,2,1,0:T(8,128)}, f32[5,4,48,128]{3,2,1,0:T(8,128)}, u32[]{:S(2)}, u32[]{:S(2)}) collective-permute-start(f32[5,4,48,128]{3,2,1,0:T(8,128)} %copy.204), channel_id=1, source_target_pairs={{0,1},{1,2},{2,3},{3,4},{4,5},{5,6},{6,7},{7,8},{8,9},{9,10},{10,1... | collective-permute-start | bytes 1474568 | tf_op jit(solution)/shard_map/ppermute | solution.py:22
  143.1 2.5 %copy.202 = f32[5,4,48,128]{3,2,1,0:T(8,128)} copy(f32[5,4,48,128]{2,1,3,0:T(4,128)} %get-tuple-element.22) | data formatting | bytes 983040 | tf_op jit(solution)/shard_map/slice | solution.py:25
  150.0 11.5 %collective-permute-done.7 = f32[5,8,4,128]{3,1,2,0:T(8,128)S(1)} collective-permute-done((f32[5,8,4,128]{3,1,2,0:T(8,128)S(1)}, f32[5,8,4,128]{3,1,2,0:T(8,128)S(1)}, u32[]{:S(2)}, u32[]{:S(2)}) %collective-permute-start.7) | collective-permute-done | bytes 81952 | tf_op jit(solution)/shard_map/ppermute | solution.py:32
  167.8 2.6 %copy.203 = f32[5,4,48,128]{2,1,3,0:T(4,128)} copy(f32[5,4,48,128]{3,2,1,0:T(8,128)} %collective-permute-done.8) | data formatting | bytes 983040 | tf_op jit(solution)/shard_map/ppermute | solution.py:25
  170.4 10.5 %broadcast_multiply_fusion = (f32[5,8,48,128]{2,1,3,0:T(8,128)}, f32[5,8,48,128]{2,1,3,0:T(8,128)}) fusion(f32[5,8,48,128]{2,1,3,0:T(8,128)S(1)} %multiply_add_fusion.1, f32[5,4,48,128]{2,1,3,0:T(4,128)} %copy.205, f32[5,4,48,128]{2,1,3,0:T(4,128)} %copy.203), kind=kLoop, calls=%fused_computation.146 | loop fusion | flops 4915200 | bytes 3932160 | tf_op jit(solution)/shard_map/mul | solution.py:69
  180.9 13.3 %multiply_add_fusion = (f32[5,8,48,128]{2,1,3,0:T(8,128)S(1)}, f32[5,8,48,128]{2,1,3,0:T(8,128)}, f32[5,8,48,128]{2,1,3,0:T(8,128)}) fusion(f32[5,8,48,128]{2,1,3,0:T(8,128)} %get-tuple-element.6, f32[8,48,128]{1,0,2:T(8,128)S(1)} %copy-done.13, f32[8,48,128]{1,0,2:T(8,128)S(1)} %copy-done.14, f32[8,48,128]{1,0,2:T(8,128)S(1)} %copy-done.12, ...), kind=kLoop, calls=%fused_computation.140 | loop fusion | flops 10813440 | bytes 5730496 | tf_op jit(solution)/shard_map/add | solution.py:74
  199.4 2.8 %fusion.105 = f32[5,8,48,128]{2,1,3,0:T(8,128)S(1)} fusion(f32[5,8,48,128]{2,1,3,0:T(8,128)S(1)} %fusion.125, f32[8,56,128]{1,0,2:T(8,128)S(1)} %fusion.113, f32[8,48,136]{1,0,2:T(8,128)S(1)} %copy-done.1, f32[5,8,48,128]{2,1,3,0:T(8,128)S(1)} %get-tuple-element.7, f32[5,8,48,128]{2,1,3,0:T(8,128)S(1)} %multiply_add_fusion.1, ...), kind=kLoop, calls=%fused_computation.183 | loop fusion | flops 2998272 | bytes 18023936 | tf_op jit(solution)/shard_map/stack | solution.py:81
  (107 shorter events, 72.2 us)
Async XLA Ops:
  2.2 37.2 %collective-permute-start.4 = (f32[5,4,48,128]{3,2,1,0:T(8,128)}, f32[5,4,48,128]{3,2,1,0:T(8,128)}, u32[]{:S(2)}, u32[]{:S(2)}) collective-permute-start(f32[5,4,48,128]{3,2,1,0:T(8,128)} %get-tuple-element.46), channel_id=1, source_target_pairs={{0,1},{1,2},{2,3},{3,4},{4,5},{5,6},{6,7},{7,8},{8,9},{9,10},{10,1... | collective-permute-start | bytes 1474568 | tf_op jit(solution)/shard_map/ppermute | solution.py:22
  7.2 33.5 %collective-permute-start.3 = (f32[5,4,48,128]{3,2,1,0:T(8,128)}, f32[5,4,48,128]{3,2,1,0:T(8,128)}, u32[]{:S(2)}, u32[]{:S(2)}) collective-permute-start(f32[5,4,48,128]{3,2,1,0:T(8,128)} %get-tuple-element.47), channel_id=1, source_target_pairs={{1,0},{2,1},{3,2},{4,3},{5,4},{6,5},{7,6},{8,7},{9,8},{10,9},{11,1... | collective-permute-start | bytes 1474568 | tf_op jit(solution)/shard_map/ppermute | solution.py:25
  11.4 107.0 %copy-start = (f32[5,8,48,128]{2,1,3,0:T(8,128)}, f32[5,8,48,128]{2,1,3,0:T(8,128)S(1)}, u32[]{:S(2)}) copy-start(f32[5,8,48,128]{2,1,3,0:T(8,128)S(1)} %copy.167) | copy-start | bytes 2949124
  11.4 12.1 %copy-start.17 = (f32[5,8,4,128]{3,2,1,0:T(4,128)S(1)}, f32[5,8,4,128]{3,2,1,0:T(4,128)}, u32[]{:S(2)}) copy-start(f32[5,8,4,128]{3,2,1,0:T(4,128)} %param.6) | copy-start | bytes 245764
  11.5 22.3 %collective-permute-start.1 = (f32[5,8,48,4]{2,1,3,0:T(8,128)S(1)}, f32[5,8,48,4]{2,1,3,0:T(8,128)S(1)}, u32[]{:S(2)}, u32[]{:S(2)}) collective-permute-start(f32[5,8,48,4]{2,1,3,0:T(8,128)S(1)} %get-tuple-element.25), channel_id=1, source_target_pairs={{0,16},{16,32},{32,48},{48,64},{64,80},{80,96},{96,112},{112,128},... | collective-permute-start | bytes 92168 | tf_op jit(solution)/shard_map/ppermute | solution.py:22
  11.5 22.2 %collective-permute-start = (f32[5,8,48,4]{2,1,3,0:T(8,128)S(1)}, f32[5,8,48,4]{2,1,3,0:T(8,128)S(1)}, u32[]{:S(2)}, u32[]{:S(2)}) collective-permute-start(f32[5,8,48,4]{2,1,3,0:T(8,128)S(1)} %get-tuple-element.24), channel_id=1, source_target_pairs={{16,0},{32,16},{48,32},{64,48},{80,64},{96,80},{112,96},{128,112},... | collective-permute-start | bytes 92168 | tf_op jit(solution)/shard_map/ppermute | solution.py:25
  17.8 16.8 %collective-permute-start.2 = (f32[5,8,4,128]{3,1,2,0:T(8,128)S(1)}, f32[5,8,4,128]{3,1,2,0:T(8,128)S(1)}, u32[]{:S(2)}, u32[]{:S(2)}) collective-permute-start(f32[5,8,4,128]{3,1,2,0:T(8,128)S(1)} %copy.209), channel_id=1, source_target_pairs={{0,128},{16,144},{32,160},{48,176},{64,192},{80,208},{96,224},{112... | collective-permute-start | bytes 245768 | tf_op jit(solution)/shard_map/ppermute | solution.py:32
  22.4 60.4 %copy-start.20 = (f32[48]{0:T(128)}, f32[48]{0:T(128)S(1)}, u32[]{:S(2)}) copy-start(f32[48]{0:T(128)S(1)} %sine_divide_fusion) | copy-start | bytes 580
  23.5 11.2 %copy-start.19 = (f32[5]{0:T(128)S(1)}, f32[5]{0:T(128)}, u32[]{:S(2)}) copy-start(f32[5]{0:T(128)} %constant.16.clone) | copy-start | bytes 64
  37.1 3.5 %copy-start.6 = (f32[5,8,48,128]{3,2,1,0:T(8,128)S(1)}, f32[5,8,48,128]{3,2,1,0:T(8,128)}, u32[]{:S(2)}) copy-start(f32[5,8,48,128]{3,2,1,0:T(8,128)} %param.5) | copy-start | bytes 2949124
  82.8 15.5 %copy-start.9 = (f32[5,8,48,128]{2,1,3,0:T(8,128)S(1)}, f32[5,8,48,128]{2,1,3,0:T(8,128)}, u32[]{:S(2)}) copy-start(f32[5,8,48,128]{2,1,3,0:T(8,128)} %get-tuple-element.12) | copy-start | bytes 2949124
  98.3 5.5 %copy-start.7 = (f32[5,8,48,128]{2,1,3,0:T(8,128)}, f32[5,8,48,128]{2,1,3,0:T(8,128)S(1)}, u32[]{:S(2)}) copy-start(f32[5,8,48,128]{2,1,3,0:T(8,128)S(1)} %get-tuple-element.14) | copy-start | bytes 2949124
  106.7 11.8 %copy-start.18 = (f32[8]{0:T(128)S(1)}, f32[8]{0:T(128)}, u32[]{:S(2)}) copy-start(f32[8]{0:T(128)} %param.7) | copy-start | bytes 100
  129.7 19.4 %collective-permute-start.6 = (f32[5,8,48,4]{2,1,3,0:T(8,128)S(1)}, f32[5,8,48,4]{2,1,3,0:T(8,128)S(1)}, u32[]{:S(2)}, u32[]{:S(2)}) collective-permute-start(f32[5,8,48,4]{2,1,3,0:T(8,128)S(1)} %get-tuple-element.18), channel_id=1, source_target_pairs={{0,16},{16,32},{32,48},{48,64},{64,80},{80,96},{96,112},{112,128},... | collective-permute-start | bytes 92168 | tf_op jit(solution)/shard_map/ppermute | solution.py:22
  129.8 19.3 %collective-permute-start.5 = (f32[5,8,48,4]{2,1,3,0:T(8,128)S(1)}, f32[5,8,48,4]{2,1,3,0:T(8,128)S(1)}, u32[]{:S(2)}, u32[]{:S(2)}) collective-permute-start(f32[5,8,48,4]{2,1,3,0:T(8,128)S(1)} %get-tuple-element.17), channel_id=1, source_target_pairs={{16,0},{32,16},{48,32},{64,48},{80,64},{96,80},{112,96},{128,112},... | collective-permute-start | bytes 92168 | tf_op jit(solution)/shard_map/ppermute | solution.py:25
  138.8 26.5 %collective-permute-start.9 = (f32[5,4,48,128]{3,2,1,0:T(8,128)}, f32[5,4,48,128]{3,2,1,0:T(8,128)}, u32[]{:S(2)}, u32[]{:S(2)}) collective-permute-start(f32[5,4,48,128]{3,2,1,0:T(8,128)} %copy.204), channel_id=1, source_target_pairs={{0,1},{1,2},{2,3},{3,4},{4,5},{5,6},{6,7},{7,8},{8,9},{9,10},{10,1... | collective-permute-start | bytes 1474568 | tf_op jit(solution)/shard_map/ppermute | solution.py:22
  145.6 22.2 %collective-permute-start.8 = (f32[5,4,48,128]{3,2,1,0:T(8,128)}, f32[5,4,48,128]{3,2,1,0:T(8,128)}, u32[]{:S(2)}, u32[]{:S(2)}) collective-permute-start(f32[5,4,48,128]{3,2,1,0:T(8,128)} %copy.202), channel_id=1, source_target_pairs={{1,0},{2,1},{3,2},{4,3},{5,4},{6,5},{7,6},{8,7},{9,8},{10,9},{11,1... | collective-permute-start | bytes 1474568 | tf_op jit(solution)/shard_map/ppermute | solution.py:25
  148.3 13.1 %collective-permute-start.7 = (f32[5,8,4,128]{3,1,2,0:T(8,128)S(1)}, f32[5,8,4,128]{3,1,2,0:T(8,128)S(1)}, u32[]{:S(2)}, u32[]{:S(2)}) collective-permute-start(f32[5,8,4,128]{3,1,2,0:T(8,128)S(1)} %copy.200), channel_id=1, source_target_pairs={{0,128},{16,144},{32,160},{48,176},{64,192},{80,208},{96,224},{112... | collective-permute-start | bytes 245768 | tf_op jit(solution)/shard_map/ppermute | solution.py:32
  170.4 10.5 %copy-start.2 = (f32[5,8,4,128]{2,1,3,0:T(8,128)S(1)}, f32[5,8,4,128]{2,1,3,0:T(8,128)}, u32[]{:S(2)}) copy-start(f32[5,8,4,128]{2,1,3,0:T(8,128)} %copy.172) | copy-start | bytes 245764
  170.4 10.5 %copy-start.3 = (f32[5,8,4,128]{2,1,3,0:T(8,128)S(1)}, f32[5,8,4,128]{2,1,3,0:T(8,128)}, u32[]{:S(2)}) copy-start(f32[5,8,4,128]{2,1,3,0:T(8,128)} %copy.201) | copy-start | bytes 245764
  170.4 10.5 %copy-start.12 = (f32[8,48,128]{1,0,2:T(8,128)S(1)}, f32[8,48,128]{1,0,2:T(8,128)}, u32[]{:S(2)}) copy-start(f32[8,48,128]{1,0,2:T(8,128)} %get-tuple-element.19) | copy-start | bytes 589828
  170.4 10.5 %copy-start.13 = (f32[8,48,128]{1,0,2:T(8,128)S(1)}, f32[8,48,128]{1,0,2:T(8,128)}, u32[]{:S(2)}) copy-start(f32[8,48,128]{1,0,2:T(8,128)} %get-tuple-element.20) | copy-start | bytes 589828
  170.4 10.5 %copy-start.14 = (f32[8,48,128]{1,0,2:T(8,128)S(1)}, f32[8,48,128]{1,0,2:T(8,128)}, u32[]{:S(2)}) copy-start(f32[8,48,128]{1,0,2:T(8,128)} %get-tuple-element.21) | copy-start | bytes 589828
  170.4 10.5 %copy-start.21 = (f32[48]{0:T(128)S(1)}, f32[48]{0:T(128)}, u32[]{:S(2)}) copy-start(f32[48]{0:T(128)} %copy-done.20) | copy-start | bytes 580
  (8 other events, 17.1 us)
where the time goes:
time: 210 us; the launch traced here: 206 us
  other arithmetic  81.7 us (39%)
  local copies, waits for them, and re-layouts  77.3 us (37%)
  starting transfers between devices  27.3 us (13%)
  waiting for transfers between devices  19.5 us (9%)
    unnamed x64, local copies, waits for them, and re-layouts  45.8 us
    add x2, other arithmetic, tendency(): wind_lon * slope_lon + wind_row * slope_row + wind_level * slope_level  28.8 us
    mul x2, other arithmetic, tendency(): slope_level = radial_ratio * first_derivative(pad_level, levels, 1)  21.1 us
    ppermute x4, starting transfers between devices, with_halo(): lax.ppermute(lax.slice_in_dim(block, 0, width, axis=dim), axis, backward)  14.5 us
    ppermute x2, waiting for transfers between devices, passed_along(): lax.ppermute(array, axis, [(i, (i + by) % peers) for i in range(peers)])  11.5 us
    unnamed x8, other arithmetic  9.68 us
    ppermute x4, starting transfers between devices, with_halo(): lax.ppermute(lax.slice_in_dim(block, block.shape[dim] - width, None, axis...  9.49 us
    another operation x2, other arithmetic, tendency(): jnp.stack([-carried[0] - spread, -carried[1] - temper * slope_lon[0] - sl...  9.29 us
  transfers between devices with their start and end apart: 10, of which 2 were waited for; matrix products, arithmetic and copies ran while one was open for 14% of the time, Pallas kernels for 0%

commit v1 on v0

v1 whole, which is shorter than its diff:
```python
import functools
import math

import jax
import jax.numpy as jnp
from jax import lax
from jax.experimental import pallas as pl
from jax.experimental.pallas import tpu as pltpu
from jax.sharding import PartitionSpec as P

first_coeffs = (0.8, -0.2, 4.0 / 105.0, -1.0 / 280.0)
second_coeffs = (-205.0 / 72.0, 1.6, -0.2, 8.0 / 315.0, -1.0 / 560.0)
time_step = 0.002
gamma_less_one = 0.4
radial_ratio = 3.0

FIELDS, LEVELS, ROWS, WIDTH = 5, 8, 48, 128
CHUNK = 8
CHUNKS = ROWS // CHUNK
LAG = 2
MESH = pl.DeviceIdType.MESH
flip = (1.0, -1.0, -1.0, 1.0, 1.0)


def placed_at(lon, rad):
    return (lon // 2) * 2 + rad % 2, (rad // 2) * 2 + lon % 2


def by_row(values, sub):
    tile = jnp.full((CHUNK, WIDTH), values[0], jnp.float32)
    for r in range(1, CHUNK):
        tile = jnp.where(sub == r, jnp.float32(values[r]), tile)
    return tile


def kernel(
    lons, rads, state, outer, kappa, out,
    home, a, b, first, total, edge_out, edge_in, pole_out, pole_in, rows_in, kap_out, kap_in,
    home_sem, in_recv, in_send, lev_recv, lev_send, edge1_recv, edge1_send, edge2_recv, edge2_send,
    pole_recv, pole_send, rows_recv, rows_send, kap_recv, kap_send, out_recv, out_send,
):
    lon, rad = lax.axis_index("lon"), lax.axis_index("rad")
    at_lon, at_rad = placed_at(lon, rad)
    swapped = at_lon != lon
    stays = at_lon == lon
    below, above = at_rad > 0, at_rad < rads - 1
    half = lons // 2

    def around(g, by):
        return lax.rem(g + by + lons, lons)

    partner = (at_lon, at_rad)
    home_right = placed_at(around(lon, 1), rad)
    home_left = placed_at(around(lon, -1), rad)
    home_across = placed_at(around(lon, half), rad)
    right = placed_at(around(at_lon, 1), at_rad)
    left = placed_at(around(at_lon, -1), at_rad)
    across = placed_at(around(at_lon, half), at_rad)
    lower = placed_at(at_lon, jnp.maximum(at_rad - 1, 0))
    upper = placed_at(at_lon, jnp.minimum(at_rad + 1, rads - 1))
    from_right = (around(at_lon, 1), at_rad)
    from_left = (around(at_lon, -1), at_rad)
    from_across = (around(at_lon, half), at_rad)

    def remote(src, dst, send, recv, to):
        return pltpu.make_async_remote_copy(
            src_ref=src, dst_ref=dst, send_sem=send, recv_sem=recv, device_id=to, device_id_type=MESH
        )

    def rows_of(i):
        return pl.ds(CHUNK * i, CHUNK)

    def ext_rows(i):
        return pl.ds(8 + CHUNK * i, CHUNK)

    own = pl.ds(4, LEVELS)

    load_home = pltpu.make_async_copy(state, home, home_sem)
    load_home.start()
    keep = [
        pltpu.make_async_copy(state.at[:, :, rows_of(i), :], a.at[:, own, ext_rows(i), :], in_recv.at[i])
        for i in range(CHUNKS)
    ]
    keep_rows = pltpu.make_async_copy(outer, rows_in, rows_recv)

    @pl.when(stays)
    def _():
        for c in keep:
            c.start()
        keep_rows.start()

    barrier = pltpu.get_barrier_semaphore()
    for peer in (home_right, home_left, home_across, right, left, across, from_right, from_left, from_across):
        pl.semaphore_signal(barrier, inc=1, device_id=peer, device_id_type=MESH)

    @pl.when(swapped)
    def _():
        pl.semaphore_signal(barrier, inc=1, device_id=partner, device_id_type=MESH)

    @pl.when(below)
    def _():
        pl.semaphore_signal(barrier, inc=1, device_id=lower, device_id_type=MESH)

    @pl.when(above)
    def _():
        pl.semaphore_signal(barrier, inc=1, device_id=upper, device_id_type=MESH)

    sub = lax.broadcasted_iota(jnp.int32, (CHUNK, WIDTH), 0)
    lane = lax.broadcasted_iota(jnp.int32, (CHUNK, WIDTH), 1)
    group = lane // 4

    def empty_levels(start):
        @pl.loop(0, 4)
        def _(l):
            for f in range(FIELDS):
                for i in range(CHUNKS):
                    a[f, start + l, ext_rows(i), :] = jnp.zeros((CHUNK, WIDTH), jnp.float32)
                    b[f, start + l, ext_rows(i), :] = jnp.zeros((CHUNK, WIDTH), jnp.float32)

    @pl.when(at_rad == 0)
    def _():
        empty_levels(0)

    @pl.when(at_rad == rads - 1)
    def _():
        empty_levels(4 + LEVELS)

    kap = jnp.full((LEVELS, WIDTH), kappa[0], jnp.float32)
    for l in range(1, LEVELS):
        kap = jnp.where(sub == l, kappa[l], kap)
    kap_out[...] = kap

    @pl.when(stays)
    def _():
        kap_in[...] = kap

    def pack(sec, i, l, tiles):
        at = lax.rem(l, 4)
        to_left = edge_out[sec, 0, i, l // 4]
        to_right = edge_out[sec, 1, i, l // 4]
        for f in range(FIELDS):
            j = 4 * f + at
            mine = group == j
            to_left = jnp.where(mine, pltpu.roll(tiles[f], 4 * j, 1), to_left)
            to_right = jnp.where(mine, pltpu.roll(tiles[f], 4 * j + 4, 1), to_right)
        edge_out[sec, 0, i, l // 4] = to_left
        edge_out[sec, 1, i, l // 4] = to_right

    def pole_rows(sec, src, level, row):
        @pl.loop(0, LEVELS)
        def _(l):
            for f in range(FIELDS):
                for k in range(4):
                    value = src[f, level + l, pl.ds(row + 3 - k, 1), :]
                    pole_out[sec, f, l, pl.ds(k, 1), :] = -value if flip[f] < 0 else value

    load_home.wait()
    edge_out[...] = jnp.zeros_like(edge_out)

    @pl.loop(0, LEVELS)
    def _(l):
        for i in range(CHUNKS):
            pack(0, i, l, [home[f, l, rows_of(i), :] for f in range(FIELDS)])

    pole_rows(0, home, 0, 0)

    pl.semaphore_wait(
        barrier, 9 + swapped.astype(jnp.int32) + below.astype(jnp.int32) + above.astype(jnp.int32)
    )

    move = [
        remote(state.at[:, :, rows_of(i), :], a.at[:, own, ext_rows(i), :], in_send.at[i], in_recv.at[i], partner)
        for i in range(CHUNKS)
    ]
    move_rows = remote(outer, rows_in, rows_send, rows_recv, partner)
    move_kap = remote(kap_out, kap_in, kap_send, kap_recv, partner)
    edges1 = [
        remote(edge_out.at[0, 0], edge_in.at[0, 1], edge1_send.at[0], edge1_recv.at[1], home_left),
        remote(edge_out.at[0, 1], edge_in.at[0, 0], edge1_send.at[1], edge1_recv.at[0], home_right),
    ]
    poles = [
        remote(pole_out.at[0], pole_in.at[0], pole_send.at[0], pole_recv.at[0], home_across),
        remote(pole_out.at[1], pole_in.at[1], pole_send.at[1], pole_recv.at[1], across),
    ]

    def halo(sec, i, src, down_level, ext):
        buffer = a if sec == 0 else b
        rows = ext_rows(i) if ext else rows_of(i)
        down = remote(
            src.at[:, pl.ds(down_level, 4), rows, :], buffer.at[:, pl.ds(4 + LEVELS, 4), ext_rows(i), :],
            lev_send.at[sec, 0, i], lev_recv.at[sec, 1, i], lower,
        )
        up = remote(
            src.at[:, pl.ds(down_level + 4, 4), rows, :], buffer.at[:, pl.ds(0, 4), ext_rows(i), :],
            lev_send.at[sec, 1, i], lev_recv.at[sec, 0, i], upper,
        )
        return down, up

    def send_levels(sec, i, src, level, ext):
        down, up = halo(sec, i, src, level, ext)

        @pl.when(below)
        def _():
            down.start()

        @pl.when(above)
        def _():
            up.start()

    def await_levels(sec, i):
        down, up = halo(sec, i, a if sec == 0 else b, 4, True)

        @pl.when(below)
        def _():
            up.wait_recv()

        @pl.when(above)
        def _():
            down.wait_recv()

    @pl.when(swapped)
    def _():
        move[0].start()
        move[1].start()

    for c in edges1:
        c.start()
    poles[0].start()

    @pl.when(swapped)
    def _():
        move_kap.start()
        for c in move[2:]:
            c.start()
        move_rows.start()

    @pl.when(stays)
    def _():
        for i in range(CHUNKS):
            send_levels(0, i, state, 0, False)

    spacing = 2.0 * math.pi / (WIDTH * lons)

    def slopes(src, sec, i, l, metric):
        at = lax.rem(l, 4)
        from_l = edge_in[sec, 0, i, l // 4]
        from_r = edge_in[sec, 1, i, l // 4]
        row = 8 + CHUNK * i
        cells, by_lon, by_rows, by_level = [], [], [], []
        second = None
        for f in range(FIELDS):
            j = 4 * f + at
            q = src[f, l + 4, ext_rows(i), :]
            beyond = jnp.where(
                lane < 64, pltpu.roll(from_r, WIDTH - 4 * j, 1), pltpu.roll(from_l, WIDTH - 4 - 4 * j, 1)
            )
            d_lon = d_row = d_lev = e_lon = e_row = e_lev = None
            for k in range(1, 5):
                c = first_coeffs[k - 1]
                ahead = pltpu.roll(jnp.where(lane >= k, q, beyond), WIDTH - k, 1)
                behind = pltpu.roll(jnp.where(lane < WIDTH - k, q, beyond), k, 1)
                south = src[f, l + 4, pl.ds(row + k, CHUNK), :]
                north = src[f, l + 4, pl.ds(row - k, CHUNK), :]
                over = src[f, l + 4 + k, ext_rows(i), :]
                under = src[f, l + 4 - k, ext_rows(i), :]
                terms = (c * (ahead - behind), c * (south - north), (radial_ratio * c) * (over - under))
                d_lon, d_row, d_lev = terms if k == 1 else (d_lon + terms[0], d_row + terms[1], d_lev + terms[2])
                if f == 4:
                    e = second_coeffs[k]
                    terms = (e * (ahead + behind), e * (south + north), e * (over + under))
                    e_lon, e_row, e_lev = (
                        terms if k == 1 else (e_lon + terms[0], e_row + terms[1], e_lev + terms[2])
                    )
            if f == 4:
                middle = second_coeffs[0] * q
                second = (e_lon + middle, e_row + middle, e_lev + middle)
            cells.append(q)
            by_lon.append(metric * d_lon)
            by_rows.append(d_row)
            by_level.append(d_lev)
        return cells, by_lon, by_rows, by_level, second

    def tendency(src, sec, i, l, metric, curvature):
        cells, by_lon, by_rows, by_level, second = slopes(src, sec, i, l, metric)
        _, u_lon, u_row, u_lev, temper = cells
        carried = [u_lon * by_lon[f] + u_row * by_rows[f] + u_lev * by_level[f] for f in range(FIELDS)]
        spread = by_lon[1] + by_rows[2] + by_level[3] + curvature * u_row
        laplace = metric * metric * second[0] + second[1] + (radial_ratio * radial_ratio) * second[2]
        kap_l = jnp.broadcast_to(kap_in[pl.ds(l, 1), :], (CHUNK, WIDTH))
        return cells, [
            -carried[0] - spread,
            -carried[1] - temper * by_lon[0] - by_lon[4],
            -carried[2] - temper * by_rows[0] - by_rows[4],
            -carried[3] - temper * by_level[0] - by_level[4],
            -carried[4] - gamma_less_one * temper * spread + kap_l * laplace,
        ]

    def geometry(i):
        thetas = [(CHUNK * i + r + 0.5) * spacing for r in range(CHUNK)]
        return by_row([1.0 / math.sin(t) for t in thetas], sub), by_row(
            [math.cos(t) / math.sin(t) for t in thetas], sub
        )

    def first_section(i):
        metric, curvature = geometry(i)

        @pl.loop(0, LEVELS)
        def _(l):
            cells, rate = tendency(a, 0, i, l, metric, curvature)
            new = []
            for f in range(FIELDS):
                first[f, l, rows_of(i), :] = rate[f]
                new.append(cells[f] + time_step * rate[f])
                b[f, l + 4, ext_rows(i), :] = new[f]
            pack(1, i, l, new)

    def second_section(i):
        metric, curvature = geometry(i)

        @pl.loop(0, LEVELS)
        def _(l):
            _, rate = tendency(b, 1, i, l, metric, curvature)
            for f in range(FIELDS):
                total[f, l, rows_of(i), :] = (0.5 * time_step) * (first[f, l, rows_of(i), :] + rate[f])

    def edges2(i):
        return (
            remote(edge_out.at[1, 0, i], edge_in.at[1, 1, i], edge2_send.at[0, i], edge2_recv.at[1, i], left),
            remote(edge_out.at[1, 1, i], edge_in.at[1, 0, i], edge2_send.at[1, i], edge2_recv.at[0, i], right),
        )

    def take_pole(sec, dst):
        poles[sec].wait_recv()

        @pl.loop(0, LEVELS)
        def _(l):
            for f in range(FIELDS):
                dst[f, l + 4, pl.ds(4, 4), :] = pole_in[sec, f, l]

    give = [
        remote(total.at[:, :, rows_of(i), :], out.at[:, :, rows_of(i), :], out_send.at[i], out_recv.at[i], partner)
        for i in range(CHUNKS)
    ]
    put = [
        pltpu.make_async_copy(total.at[:, :, rows_of(i), :], out.at[:, :, rows_of(i), :], out_send.at[i])
        for i in range(CHUNKS)
    ]

    for t in range(CHUNKS + 1 + LAG):
        if t < CHUNKS:

            @pl.when(swapped)
            def _():
                move[t].wait_recv()
                send_levels(0, t, a, 4, True)

            @pl.when(stays)
            def _():
                keep[t].wait()

        i = t - 1
        if i == 0:
            for c in edges1:
                c.wait_recv()
            take_pole(0, a)

            @pl.when(swapped)
            def _():
                move_kap.wait_recv()

        if i == CHUNKS - 1:

            @pl.when(swapped)
            def _():
                move_rows.wait_recv()

            @pl.when(stays)
            def _():
                keep_rows.wait()

            @pl.loop(0, LEVELS)
            def _(l):
                for f in range(FIELDS):
                    a[f, l + 4, pl.ds(8 + ROWS, 4), :] = rows_in[f, l]
                    b[f, l + 4, pl.ds(8 + ROWS, 4), :] = rows_in[f, l]

        if 0 <= i < CHUNKS:
            await_levels(0, i)
            first_section(i)
            if i == 0:
                pole_rows(1, b, 4, 8)
                poles[1].start()
            send_levels(1, i, b, 4, True)
            for c in edges2(i):
                c.start()
        i = t - 1 - LAG
        if 0 <= i < CHUNKS:
            if i == 0:
                take_pole(1, b)
            await_levels(1, i)
            for c in edges2(i):
                c.wait_recv()
            second_section(i)

            @pl.when(swapped)
            def _():
                give[i].start()

            @pl.when(stays)
            def _():
                put[i].start()

    for c in (*edges1, *poles):
        c.wait_send()
    for i in range(CHUNKS):
        for c in edges2(i):
            c.wait_send()
        for sec in range(2):
            down, up = halo(sec, i, a if sec == 0 else b, 4, True)

            @pl.when(below)
            def _():
                down.wait_send()

            @pl.when(above)
            def _():
                up.wait_send()

    @pl.when(stays)
    def _():
        for c in put:
            c.wait()

    @pl.when(swapped)
    def _():
        for c in (*move, move_rows, move_kap):
            c.wait_send()
        for c in give:
            c.wait()


def solution(mesh):
    lons, rads = mesh.shape["lon"], mesh.shape["rad"]

    def on_device(state, outer_rows, kappa):
        f32 = jnp.float32
        vmem, dma = pltpu.VMEM, pltpu.SemaphoreType.DMA
        block = (FIELDS, LEVELS, ROWS, WIDTH)
        wide = (FIELDS, LEVELS + 8, ROWS + 16, WIDTH)
        edges = (2, 2, CHUNKS, 2, CHUNK, WIDTH)
        pole = (2, FIELDS, LEVELS, 4, WIDTH)
        return pl.pallas_call(
            functools.partial(kernel, lons, rads),
            out_shape=jax.ShapeDtypeStruct(block, f32),
            in_specs=[
                pl.BlockSpec(memory_space=pl.ANY),
                pl.BlockSpec(memory_space=pl.ANY),
                pl.BlockSpec(memory_space=pltpu.SMEM),
            ],
            out_specs=pl.BlockSpec(memory_space=pl.ANY),
            scratch_shapes=[
                vmem(block, f32), vmem(wide, f32), vmem(wide, f32), vmem(block, f32), vmem(block, f32),
                vmem(edges, f32), vmem(edges, f32), vmem(pole, f32), vmem(pole, f32),
                vmem((FIELDS, LEVELS, 4, WIDTH), f32), vmem((LEVELS, WIDTH), f32), vmem((LEVELS, WIDTH), f32),
                dma, dma((CHUNKS,)), dma((CHUNKS,)), dma((2, 2, CHUNKS)), dma((2, 2, CHUNKS)),
                dma((2,)), dma((2,)), dma((2, CHUNKS)), dma((2, CHUNKS)),
                dma((2,)), dma((2,)), dma, dma, dma, dma, dma((CHUNKS,)), dma((CHUNKS,)),
            ],
            compiler_params=pltpu.CompilerParams(
                collective_id=0, has_side_effects=True, vmem_limit_bytes=48 * 1024 * 1024
            ),
        )(state, outer_rows, kappa)

    placed = (P(None, "rad", None, "lon"), P(None, "rad", None, "lon"), P("rad"))
    return jax.shard_map(
        on_device, mesh=mesh, in_specs=placed, out_specs=P(None, "rad", None, "lon"), check_vma=False
    )
```

time: 210 us -> 49.2 us (0.23); the launches traced: 206 us -> 48.4 us
  other arithmetic: 81.7 us -> 0 us
  local copies, waits for them, and re-layouts: 77.3 us -> 3.69 us
  Pallas kernels: 0 us -> 44.7 us
  starting transfers between devices: 27.3 us -> 0 us
  waiting for transfers between devices: 19.5 us -> 0 us
    pallas_call x0 -> x1, Pallas kernels: none -> 44.7 us  [on_device(): pl.pallas_call(functools.partial(kernel, lons, rads), out_shape=jax.Shape...]
    unnamed x64 -> x7, local copies, waits for them, and re-layouts: 45.8 us -> 3.69 us
    add x3 -> x0, other arithmetic: 31.6 us -> none  [the longest x2 28.8 us: tendency(): wind_lon * slope_lon + wind_row * slope_row + wind_level * slope_level]
    ppermute x10 -> x0, starting transfers between devices: 27.3 us -> none  [the longest x4 14.5 us: with_halo(): lax.ppermute(lax.slice_in_dim(block, 0, width, axis=dim), axis, backward)]
    mul x8 -> x0, other arithmetic: 25.6 us -> none  [the longest x2 21.1 us: tendency(): slope_level = radial_ratio * first_derivative(pad_level, levels, 1)]
    ppermute x10 -> x0, waiting for transfers between devices: 19.5 us -> none  [the longest x2 11.5 us: passed_along(): lax.ppermute(array, axis, [(i, (i + by) % peers) for i in range(peers)])]
    slice x12 -> x0, local copies, waits for them, and re-layouts: 16.7 us -> none  [the longest x4 5.82 us: window(): return lax.slice_in_dim(padded, offset, offset + length, axis=axis)]
    unnamed x8 -> x0, other arithmetic: 9.68 us -> none
  transfers between devices with their start and end apart: 10 -> 0, of which waited for: 2 -> 0; matrix products, arithmetic and copies ran while one was open for 14% -> 0% of each run, Pallas kernels for 0% -> 0%
where the time goes in v1:
time: 49.2 us; the launch traced here: 48.4 us
  Pallas kernels  44.7 us (91%)
  local copies, waits for them, and re-layouts  3.69 us (8%)
    pallas_call x1, Pallas kernels, on_device(): pl.pallas_call(functools.partial(kernel, lons, rads), out_shape=jax.Shape...  44.7 us
    unnamed x7, local copies, waits for them, and re-layouts  3.69 us

profile of v1, /device:TPU:98, one launch (start us, length us, event | category | flops | bytes accessed | tf_op | source)
XLA Modules:
  0.0 48.4 jit_solution(18265296798939521458)
XLA Ops:
  0.0 0.0 copy-start
  0.0 1.2 %copy-done = f32[5,8,48,128]{3,2,1,0:T(8,128)S(1)} copy-done((f32[5,8,48,128]{3,2,1,0:T(8,128)S(1)}, f32[5,8,48,128]{3,2,1,0:T(8,128)}, u32[]{:S(2)}) %copy-start) | copy-done | bytes 983064
  1.2 0.0 copy-start.1
  1.2 0.9 %copy-done.1 = f32[5,8,4,128]{3,2,1,0:T(4,128)S(1)} copy-done((f32[5,8,4,128]{3,2,1,0:T(4,128)S(1)}, f32[5,8,4,128]{3,2,1,0:T(4,128)}, u32[]{:S(2)}) %copy-start.1) | copy-done | bytes 81944
  2.1 0.0 copy-start.2
  2.1 0.7 %copy-done.2 = f32[8]{0:T(128)S(1)} copy-done((f32[8]{0:T(128)S(1)}, f32[8]{0:T(128)}, u32[]{:S(2)}) %copy-start.2) | copy-done | bytes 56
  2.7 44.7 %shard_map.37 = f32[5,8,48,128]{3,2,1,0:T(8,128)S(1)} custom-call(f32[5,8,48,128]{3,2,1,0:T(8,128)S(1)} %copy-done, f32[5,8,4,128]{3,2,1,0:T(4,128)S(1)} %copy-done.1, f32[8]{0:T(128)S(1)} %copy-done.2), custom_call_target="tpu_custom_call" | custom-call | tf_op jit(solution)/shard_map/pallas_call | solution.py:452
  47.5 0.9 %copy.5 = f32[5,8,48,128]{3,2,1,0:T(8,128)} copy(f32[5,8,48,128]{3,2,1,0:T(8,128)S(1)} %shard_map.37) | data formatting | bytes 1966080
Async XLA Ops:
  0.0 1.2 %copy-start = (f32[5,8,48,128]{3,2,1,0:T(8,128)S(1)}, f32[5,8,48,128]{3,2,1,0:T(8,128)}, u32[]{:S(2)}) copy-start(f32[5,8,48,128]{3,2,1,0:T(8,128)} %state.1) | copy-start | bytes 2949124
  1.2 0.9 %copy-start.1 = (f32[5,8,4,128]{3,2,1,0:T(4,128)S(1)}, f32[5,8,4,128]{3,2,1,0:T(4,128)}, u32[]{:S(2)}) copy-start(f32[5,8,4,128]{3,2,1,0:T(4,128)} %outer.1) | copy-start | bytes 245764
  2.1 0.7 %copy-start.2 = (f32[8]{0:T(128)S(1)}, f32[8]{0:T(128)}, u32[]{:S(2)}) copy-start(f32[8]{0:T(128)} %kappa.1) | copy-start | bytes 100

commit v2 on v1

v2 whole, which is shorter than its diff:
```python
import functools
import math

import jax
import jax.numpy as jnp
from jax import lax
from jax.experimental import pallas as pl
from jax.experimental.pallas import tpu as pltpu
from jax.sharding import PartitionSpec as P

first_coeffs = (0.8, -0.2, 4.0 / 105.0, -1.0 / 280.0)
second_coeffs = (-205.0 / 72.0, 1.6, -0.2, 8.0 / 315.0, -1.0 / 560.0)
time_step = 0.002
gamma_less_one = 0.4
radial_ratio = 3.0

FIELDS, LEVELS, ROWS, WIDTH = 5, 8, 48, 128
CHUNK = 8
CHUNKS = ROWS // CHUNK
LAG = 3
AHEAD = 4
UNROLL, UNROLL_LON = 2, 4
MESH = pl.DeviceIdType.MESH
flip = (1.0, -1.0, -1.0, 1.0, 1.0)


def placed_at(lon, rad, lons):
    odd = ((lon // 2) % (lons // 4) + lon // (lons // 2)) % 2
    return (lon // 2) * 2 + (rad + odd) % 2, (rad // 2) * 2 + (lon + odd) % 2


def by_row(values, sub):
    tile = jnp.full((CHUNK, WIDTH), values[0], jnp.float32)
    for r in range(1, CHUNK):
        tile = jnp.where(sub == r, jnp.float32(values[r]), tile)
    return tile


def kernel(
    lons, rads, state, outer, kappa, out,
    a, b, first, total, along, edge_own, edge_out, edge_in, pole_out, pole_in, rows_in, kap_out, kap_in, kap_s,
    kap_sem, in_recv, in_send, lev_recv, lev_send, edge_recv, edge_send,
    pole_recv, pole_send, rows_recv, rows_send, kap_recv, kap_send, out_recv, out_send,
):
    lon, rad = lax.axis_index("lon"), lax.axis_index("rad")
    at_lon, at_rad = placed_at(lon, rad, lons)
    swapped = at_lon != lon
    stays = at_lon == lon
    below, above = at_rad > 0, at_rad < rads - 1
    half = lons // 2

    def around(g, by):
        return lax.rem(g + by + lons, lons)

    partner = (at_lon, at_rad)
    right = placed_at(around(at_lon, 1), at_rad, lons)
    left = placed_at(around(at_lon, -1), at_rad, lons)
    across = placed_at(around(at_lon, half), at_rad, lons)
    lower = placed_at(at_lon, jnp.maximum(at_rad - 1, 0), lons)
    upper = placed_at(at_lon, jnp.minimum(at_rad + 1, rads - 1), lons)
    def remote(src, dst, send, recv, to):
        return pltpu.make_async_remote_copy(
            src_ref=src, dst_ref=dst, send_sem=send, recv_sem=recv, device_id=to, device_id_type=MESH
        )

    def rows_of(i):
        return pl.ds(CHUNK * i, CHUNK)

    def ext_rows(i):
        return pl.ds(8 + CHUNK * i, CHUNK)

    own = pl.ds(4, LEVELS)

    load_kap = pltpu.make_async_copy(kappa, kap_s, kap_sem)
    keep = [
        pltpu.make_async_copy(state.at[:, :, rows_of(i), :], a.at[:, own, ext_rows(i), :], in_recv.at[i])
        for i in range(CHUNKS)
    ]
    keep_rows = pltpu.make_async_copy(outer, rows_in, rows_recv)

    barrier = pltpu.get_barrier_semaphore()
    for peer in (right, left, across):
        pl.semaphore_signal(barrier, inc=1, device_id=peer, device_id_type=MESH)

    @pl.when(swapped)
    def _():
        pl.semaphore_signal(barrier, inc=1, device_id=partner, device_id_type=MESH)

    @pl.when(below)
    def _():
        pl.semaphore_signal(barrier, inc=1, device_id=lower, device_id_type=MESH)

    @pl.when(above)
    def _():
        pl.semaphore_signal(barrier, inc=1, device_id=upper, device_id_type=MESH)

    load_kap.start()

    @pl.when(stays)
    def _():
        for c in keep:
            c.start()
        keep_rows.start()

    sub = lax.broadcasted_iota(jnp.int32, (CHUNK, WIDTH), 0)
    lane = lax.broadcasted_iota(jnp.int32, (CHUNK, WIDTH), 1)
    group = lane // 8
    low = lane % 8 < 4
    across_seam = (lane < 4) | (lane >= WIDTH - 4)

    def empty_levels(start):
        @pl.loop(0, 4)
        def _(l):
            for f in range(FIELDS):
                for i in range(CHUNKS):
                    a[f, start + l, ext_rows(i), :] = jnp.zeros((CHUNK, WIDTH), jnp.float32)
                    b[f, start + l, ext_rows(i), :] = jnp.zeros((CHUNK, WIDTH), jnp.float32)

    @pl.when(at_rad == 0)
    def _():
        empty_levels(0)

    @pl.when(at_rad == rads - 1)
    def _():
        empty_levels(4 + LEVELS)

    edge_own[...] = jnp.zeros_like(edge_own)
    load_kap.wait()
    kap = jnp.full((LEVELS, WIDTH), kap_s[0], jnp.float32)
    for l in range(1, LEVELS):
        kap = jnp.where(sub == l, kap_s[l], kap)
    kap = kap * (time_step * second_coeffs[1])
    kap_out[...] = kap

    @pl.when(stays)
    def _():
        kap_in[...] = kap

    def put_edges(held, l, tiles):
        held = list(held)
        for f in range(FIELDS):
            at = 8 * (f % 2) + l
            held[f // 2] = jnp.where(group == at, pltpu.roll(tiles[f], (8 * at + 4) % WIDTH, 1), held[f // 2])
        return held

    def packed(src, level, row):
        held = [jnp.zeros((CHUNK, WIDTH), jnp.float32)] * 3
        for l in range(LEVELS):
            held = put_edges(held, l, [src[f, level + l, pl.ds(row, CHUNK), :] for f in range(FIELDS)])
        return held

    def post_edges(sec, i, held):
        edge_out[sec, 0, i, 0] = jnp.where(low, pltpu.roll(held[1], WIDTH - 4, 1), held[0])
        edge_out[sec, 0, i, 1] = held[2]
        edge_out[sec, 1, i, 0] = jnp.where(low, held[0], pltpu.roll(held[1], 4, 1))
        edge_out[sec, 1, i, 1] = held[2]

    def pole_rows(sec, src, level, row):
        mirror = lax.rem(11 - sub, 8)

        @pl.loop(0, LEVELS)
        def _(l):
            for f in range(FIELDS):
                value = jnp.take_along_axis(src[f, level + l, pl.ds(row, CHUNK), :], mirror, axis=0)
                pole_out[sec, f, l] = (-value if flip[f] < 0 else value)[:4]

    pl.semaphore_wait(
        barrier, 3 + swapped.astype(jnp.int32) + below.astype(jnp.int32) + above.astype(jnp.int32)
    )

    move = [
        remote(state.at[:, :, rows_of(i), :], a.at[:, own, ext_rows(i), :], in_send.at[i], in_recv.at[i], partner)
        for i in range(CHUNKS)
    ]
    move_rows = remote(outer, rows_in, rows_send, rows_recv, partner)
    move_kap = remote(kap_out, kap_in, kap_send, kap_recv, partner)
    poles = [
        remote(pole_out.at[n], pole_in.at[n], pole_send.at[n], pole_recv.at[n], across) for n in range(2)
    ]

    def edges(sec, i):
        return (
            remote(edge_out.at[sec, 0, i], edge_in.at[sec, 1, i], edge_send.at[sec, 0, i], edge_recv.at[sec, 1, i], left),
            remote(edge_out.at[sec, 1, i], edge_in.at[sec, 0, i], edge_send.at[sec, 1, i], edge_recv.at[sec, 0, i], right),
        )

    def halo(sec, i, src, down_level, ext):
        buffer = a if sec == 0 else b
        rows = ext_rows(i) if ext else rows_of(i)
        down = remote(
            src.at[:, pl.ds(down_level, 4), rows, :], buffer.at[:, pl.ds(4 + LEVELS, 4), ext_rows(i), :],
            lev_send.at[sec, 0, i], lev_recv.at[sec, 1, i], lower,
        )
        up = remote(
            src.at[:, pl.ds(down_level + 4, 4), rows, :], buffer.at[:, pl.ds(0, 4), ext_rows(i), :],
            lev_send.at[sec, 1, i], lev_recv.at[sec, 0, i], upper,
        )
        return down, up

    def send_levels(sec, i, src, level, ext):
        down, up = halo(sec, i, src, level, ext)

        @pl.when(below)
        def _():
            down.start()

        @pl.when(above)
        def _():
            up.start()

    def await_levels(sec, i):
        down, up = halo(sec, i, a if sec == 0 else b, 4, True)

        @pl.when(below)
        def _():
            up.wait_recv()

        @pl.when(above)
        def _():
            down.wait_recv()

    def send_edges(sec, i, src):
        if sec == 0:
            held = packed(src, 4, 8 + CHUNK * i)
            for n in range(3):
                edge_own[0, i, n] = held[n]
        else:
            held = [edge_own[1, i, n] for n in range(3)]
        post_edges(sec, i, held)
        for c in edges(sec, i):
            c.start()
        if i == 0:
            pole_rows(sec, src, 4, 8)
            poles[sec].start()

    @pl.when(swapped)
    def _():
        move_kap.start()
        for c in move[:AHEAD]:
            c.start()

    @pl.when(stays)
    def _():
        for i in range(CHUNKS):
            send_levels(0, i, state, 0, False)
        for i in range(CHUNKS):
            keep[i].wait()
            send_edges(0, i, a)

    spacing = 2.0 * math.pi / (WIDTH * lons)

    first_ratio = [c / first_coeffs[0] for c in first_coeffs]
    second_ratio = [e / second_coeffs[1] for e in second_coeffs[1:]]
    step = time_step * first_coeffs[0]

    def weighed(terms, ratios):
        return terms[0] + ratios[1] * terms[1] + ratios[2] * terms[2] + ratios[3] * terms[3]

    def seam(sec, i, own):
        left = [edge_in[sec, 0, i, n] for n in range(2)]
        right = [edge_in[sec, 1, i, n] for n in range(2)]
        beyond = (
            jnp.where(low, left[0], right[0]),
            jnp.where(low, pltpu.roll(left[0], WIDTH - 4, 1), pltpu.roll(right[0], 4, 1)),
            jnp.where(low, left[1], right[1]),
        )
        found = []
        for n in range(3):
            lack = beyond[n] - own[n]
            on_right = jnp.where(low, 0.0, lack)
            on_left = jnp.where(low, lack, 0.0)
            ahead = [pltpu.roll(on_right, WIDTH - k, 1) for k in range(1, 5)]
            behind = [pltpu.roll(on_left, k, 1) for k in range(1, 5)]
            d = jnp.where(low, weighed(ahead, first_ratio), -weighed(behind, first_ratio))
            if n == 2:
                e = jnp.where(low, weighed(ahead, second_ratio), weighed(behind, second_ratio))
                d = jnp.where(lane < 64, d, pltpu.roll(e, 64, 1))
            found.append(d)
        return found

    def turned(q, m, d, ratios, sign):
        even = ratios[2] * q + (0.5 * (ratios[1] + ratios[3])) * m
        odd = (0.5 * (ratios[3] - ratios[1])) * d
        ahead, behind = pltpu.roll(even + odd, WIDTH - 3, 1), pltpu.roll(even - odd, 3, 1)
        return d + (ahead - behind) if sign < 0 else m + (ahead + behind)

    def along_lon(src, i, extra):
        def seam_of(n, at):
            return jnp.where(across_seam, pltpu.roll(extra[n], WIDTH - 4 - 8 * at, 1), 0.0)

        @pl.loop(0, LEVELS, unroll=UNROLL_LON)
        def _(l):
            for f in range(FIELDS):
                q = src[f, l + 4, ext_rows(i), :]
                ahead, behind = pltpu.roll(q, WIDTH - 1, 1), pltpu.roll(q, 1, 1)
                m, d = ahead + behind, ahead - behind
                along[f, l] = turned(q, m, d, first_ratio, -1) + seam_of(f // 2, 8 * (f % 2) + l)
                if f == 4:
                    along[5, l] = turned(q, m, d, second_ratio, 1) + seam_of(2, 8 + l)

    def tendency(src, i, l, consts):
        stretch, turn, stretch2, centre = consts
        row = 8 + CHUNK * i
        cells = [src[f, l + 4, ext_rows(i), :] for f in range(FIELDS)]
        _, u_lon, u_row, u_lev, temper = cells
        by_lon = [along[f, l] for f in range(FIELDS)]
        by_rows, by_level = [], []
        for f in range(FIELDS):
            row_d, lev_d, row_s, lev_s = [], [], [], []
            for k in range(1, 5):
                south = src[f, l + 4, pl.ds(row + k, CHUNK), :]
                north = src[f, l + 4, pl.ds(row - k, CHUNK), :]
                over = src[f, l + 4 + k, ext_rows(i), :]
                under = src[f, l + 4 - k, ext_rows(i), :]
                row_d.append(south - north)
                lev_d.append(over - under)
                if f == 4:
                    row_s.append(south + north)
                    lev_s.append(over + under)
            by_rows.append(weighed(row_d, first_ratio))
            by_level.append(weighed(lev_d, first_ratio))
            if f == 4:
                laplace = (
                    stretch2 * along[5, l]
                    + weighed(row_s, second_ratio)
                    + (radial_ratio * radial_ratio) * weighed(lev_s, second_ratio)
                    + centre * temper
                )
        to_lon, to_row, to_lev = stretch * u_lon, step * u_row, (radial_ratio * step) * u_lev
        carried = [to_lon * by_lon[f] + to_row * by_rows[f] + to_lev * by_level[f] for f in range(FIELDS)]
        spread = stretch * by_lon[1] + step * (by_rows[2] + radial_ratio * by_level[3]) + turn * u_row
        kap_l = jnp.broadcast_to(kap_in[pl.ds(l, 1), :], (CHUNK, WIDTH))
        return cells, [
            carried[0] + spread,
            carried[1] + stretch * (temper * by_lon[0] + by_lon[4]),
            carried[2] + step * (temper * by_rows[0] + by_rows[4]),
            carried[3] + (radial_ratio * step) * (temper * by_level[0] + by_level[4]),
            carried[4] + (gamma_less_one * temper) * spread - kap_l * laplace,
        ]

    def geometry(i):
        thetas = [(CHUNK * i + r + 0.5) * spacing for r in range(CHUNK)]
        metric = [1.0 / math.sin(t) for t in thetas]
        return (
            by_row([step * m for m in metric], sub),
            by_row([time_step * math.cos(t) * m for t, m in zip(thetas, metric)], sub),
            by_row([m * m for m in metric], sub),
            by_row([second_coeffs[0] / second_coeffs[1] * (m * m + 1 + radial_ratio**2) for m in metric], sub),
        )

    def first_section(i):
        consts = geometry(i)
        along_lon(a, i, seam(0, i, [edge_own[0, i, n] for n in range(3)]))

        @pl.loop(0, LEVELS, unroll=UNROLL)
        def _(l):
            cells, rate = tendency(a, i, l, consts)
            new = []
            for f in range(FIELDS):
                first[f, l, rows_of(i), :] = rate[f]
                new.append(cells[f] - rate[f])
                b[f, l + 4, ext_rows(i), :] = new[f]
            held = put_edges([edge_own[1, i, n] for n in range(3)], l, new)
            for n in range(3):
                edge_own[1, i, n] = held[n]

    def second_section(i):
        consts = geometry(i)
        along_lon(b, i, seam(1, i, [edge_own[1, i, n] for n in range(3)]))

        @pl.loop(0, LEVELS, unroll=UNROLL)
        def _(l):
            _, rate = tendency(b, i, l, consts)
            for f in range(FIELDS):
                total[f, l, rows_of(i), :] = -0.5 * (first[f, l, rows_of(i), :] + rate[f])

    def take_pole(sec, dst):
        poles[sec].wait_recv()

        @pl.loop(0, LEVELS)
        def _(l):
            for f in range(FIELDS):
                dst[f, l + 4, pl.ds(4, 4), :] = pole_in[sec, f, l]

    give = [
        remote(total.at[:, :, rows_of(i), :], out.at[:, :, rows_of(i), :], out_send.at[i], out_recv.at[i], partner)
        for i in range(CHUNKS)
    ]
    put = [
        pltpu.make_async_copy(total.at[:, :, rows_of(i), :], out.at[:, :, rows_of(i), :], out_send.at[i])
        for i in range(CHUNKS)
    ]

    for t in range(CHUNKS + 1 + LAG):
        if t < CHUNKS:

            @pl.when(swapped)
            def _():
                move[t].wait_recv()
                send_levels(0, t, a, 4, True)
                send_edges(0, t, a)

        i = t - 1
        if i == 0:
            take_pole(0, a)

            @pl.when(swapped)
            def _():
                move_kap.wait_recv()

        if i == CHUNKS - 1:

            @pl.when(swapped)
            def _():
                move_rows.wait_recv()

            @pl.when(stays)
            def _():
                keep_rows.wait()

            @pl.loop(0, LEVELS)
            def _(l):
                for f in range(FIELDS):
                    a[f, l + 4, pl.ds(8 + ROWS, 4), :] = rows_in[f, l]
                    b[f, l + 4, pl.ds(8 + ROWS, 4), :] = rows_in[f, l]

        if 0 <= i < CHUNKS:
            await_levels(0, i)
            for c in edges(0, i):
                c.wait_recv()
            first_section(i)
            send_levels(1, i, b, 4, True)
            send_edges(1, i, b)
        if t + AHEAD < CHUNKS:

            @pl.when(swapped)
            def _():
                move[t + AHEAD].start()
                if t + AHEAD == CHUNKS - 1:
                    move_rows.start()
        i = t - 1 - LAG
        if 0 <= i < CHUNKS:
            if i == 0:
                take_pole(1, b)
            await_levels(1, i)
            for c in edges(1, i):
                c.wait_recv()
            second_section(i)

            @pl.when(swapped)
            def _():
                give[i].start()

            @pl.when(stays)
            def _():
                put[i].start()

    for c in poles:
        c.wait_send()
    for i in range(CHUNKS):
        for sec in range(2):
            for c in edges(sec, i):
                c.wait_send()
            down, up = halo(sec, i, a if sec == 0 else b, 4, True)

            @pl.when(below)
            def _():
                down.wait_send()

            @pl.when(above)
            def _():
                up.wait_send()

    @pl.when(stays)
    def _():
        for c in put:
            c.wait()

    @pl.when(swapped)
    def _():
        for c in (*move, move_rows, move_kap):
            c.wait_send()
        for c in give:
            c.wait()


def solution(mesh):
    lons, rads = mesh.shape["lon"], mesh.shape["rad"]

    def on_device(state, outer_rows, kappa):
        f32 = jnp.float32
        vmem, dma = pltpu.VMEM, pltpu.SemaphoreType.DMA
        block = (FIELDS, LEVELS, ROWS, WIDTH)
        wide = (FIELDS, LEVELS + 8, ROWS + 16, WIDTH)
        edges = (2, 2, CHUNKS, 2, CHUNK, WIDTH)
        own_edges = (2, CHUNKS, 3, CHUNK, WIDTH)
        pole = (2, FIELDS, LEVELS, 4, WIDTH)
        return pl.pallas_call(
            functools.partial(kernel, lons, rads),
            out_shape=jax.ShapeDtypeStruct(block, f32),
            in_specs=[
                pl.BlockSpec(memory_space=pltpu.HBM),
                pl.BlockSpec(memory_space=pltpu.HBM),
                pl.BlockSpec(memory_space=pltpu.HBM),
            ],
            out_specs=pl.BlockSpec(memory_space=pl.ANY),
            scratch_shapes=[
                vmem(wide, f32), vmem(wide, f32), vmem(block, f32), vmem(block, f32),
                vmem((FIELDS + 1, LEVELS, CHUNK, WIDTH), f32),
                vmem(own_edges, f32), vmem(edges, f32), vmem(edges, f32), vmem(pole, f32), vmem(pole, f32),
                vmem((FIELDS, LEVELS, 4, WIDTH), f32), vmem((LEVELS, WIDTH), f32), vmem((LEVELS, WIDTH), f32), pltpu.SMEM((LEVELS,), f32),
                dma, dma((CHUNKS,)), dma((CHUNKS,)), dma((2, 2, CHUNKS)), dma((2, 2, CHUNKS)),
                dma((2, 2, CHUNKS)), dma((2, 2, CHUNKS)),
                dma((2,)), dma((2,)), dma, dma, dma, dma, dma((CHUNKS,)), dma((CHUNKS,)),
            ],
            compiler_params=pltpu.CompilerParams(
                collective_id=0, has_side_effects=True, vmem_limit_bytes=66_000_000
            ),
        )(state, outer_rows, kappa)

    placed = (P(None, "rad", None, "lon"), P(None, "rad", None, "lon"), P("rad"))
    return jax.shard_map(
        on_device, mesh=mesh, in_specs=placed, out_specs=P(None, "rad", None, "lon"), check_vma=False
    )
```

time: 49.2 us -> 38.1 us (0.77); the launches traced: 48.4 us -> 38 us
  Pallas kernels: 44.7 us -> 35.8 us
  local copies, waits for them, and re-layouts: 3.69 us -> 2.24 us
    pallas_call x1, Pallas kernels: 44.7 us -> 35.8 us  [on_device(): pl.pallas_call(functools.partial(kernel, lons, rads), out_shape=jax.Shape...]
    unnamed x7 -> x1, local copies, waits for them, and re-layouts: 3.69 us -> 2.24 us
where the time goes in v2:
time: 38.1 us; the launch traced here: 38 us
  Pallas kernels  35.8 us (94%)
  local copies, waits for them, and re-layouts  2.24 us (6%)
    pallas_call x1, Pallas kernels, on_device(): pl.pallas_call(functools.partial(kernel, lons, rads), out_shape=jax.Shape...  35.8 us
    unnamed x1, local copies, waits for them, and re-layouts  2.24 us

profile of v2, /device:TPU:98, one launch (start us, length us, event | category | flops | bytes accessed | tf_op | source)
XLA Modules:
  0.0 38.0 jit_solution(8398777661376907657)
XLA Ops:
  0.0 35.8 %shard_map.37 = f32[5,8,48,128]{3,2,1,0:T(8,128)} custom-call(f32[5,8,48,128]{3,2,1,0:T(8,128)} %state.1, f32[5,8,4,128]{3,2,1,0:T(4,128)} %outer.1, f32[8]{0:T(128)} %kappa.1), custom_call_target="tpu_custom_call" | custom-call | tf_op jit(solution)/shard_map/pallas_call | solution.py:498
  35.8 2.2 %copy.5 = f32[5,8,48,128]{3,2,1,0:T(8,128)} copy(f32[5,8,48,128]{3,2,1,0:T(8,128)} %shard_map.37) | data formatting | bytes 1966080

commit v3 on v2

--- a/solution.py
+++ b/solution.py
@@ -13,13 +13,15 @@
 time_step = 0.002
 gamma_less_one = 0.4
 radial_ratio = 3.0
+first_taps = (672.0, -168.0, 32.0, -3.0)
+second_taps = (8064.0, -1008.0, 128.0, -9.0)
 
 FIELDS, LEVELS, ROWS, WIDTH = 5, 8, 48, 128
 CHUNK = 8
 CHUNKS = ROWS // CHUNK
-LAG = 3
+LAG, LAG_STAYS = 3, 5
 AHEAD = 4
-UNROLL, UNROLL_LON = 2, 4
+UNROLL = 2
 MESH = pl.DeviceIdType.MESH
 flip = (1.0, -1.0, -1.0, 1.0, 1.0)
 
@@ -38,8 +40,8 @@
 
 def kernel(
     lons, rads, state, outer, kappa, out,
-    a, b, first, total, along, edge_own, edge_out, edge_in, pole_out, pole_in, rows_in, kap_out, kap_in, kap_s,
-    kap_sem, in_recv, in_send, lev_recv, lev_send, edge_recv, edge_send,
+    home, home_out, a, b, first, total, along, edge_own, edge_out, edge_in, pole_out, pole_in, rows_in, kap_out, kap_in, taps, kap_s,
+    home_sem, home_send, kap_sem, in_recv, in_send, lev_recv, lev_send, edge_recv, edge_send,
     pole_recv, pole_send, rows_recv, rows_send, kap_recv, kap_send, out_recv, out_send,
 ):
     lon, rad = lax.axis_index("lon"), lax.axis_index("rad")
@@ -48,6 +50,8 @@
     stays = at_lon == lon
     below, above = at_rad > 0, at_rad < rads - 1
     half = lons // 2
+    home_side, side_of_pair = lon % 2, at_lon % 2
+    sibling = (lon + 1 - 2 * home_side, rad)
 
     def around(g, by):
         return lax.rem(g + by + lons, lons)
@@ -71,6 +75,7 @@
 
     own = pl.ds(4, LEVELS)
 
+    load_home = pltpu.make_async_copy(state, home, home_sem)
     load_kap = pltpu.make_async_copy(kappa, kap_s, kap_sem)
     keep = [
         pltpu.make_async_copy(state.at[:, :, rows_of(i), :], a.at[:, own, ext_rows(i), :], in_recv.at[i])
@@ -95,6 +100,10 @@
         pl.semaphore_signal(barrier, inc=1, device_id=upper, device_id_type=MESH)
 
     load_kap.start()
+
+    @pl.when(swapped)
+    def _():
+        load_home.start()
 
     @pl.when(stays)
     def _():
@@ -124,7 +133,34 @@
     def _():
         empty_levels(4 + LEVELS)
 
-    edge_own[...] = jnp.zeros_like(edge_own)
+    def put_edges(held, l, tiles):
+        held = list(held)
+        for f in range(FIELDS):
+            at = 8 * (f % 2) + l
+            held[f // 2] = jnp.where(group == at, pltpu.roll(tiles[f], (8 * at + 4) % WIDTH, 1), held[f // 2])
+        return held
+
+    def packed(src, level, row):
+        held = [jnp.zeros((CHUNK, WIDTH), jnp.float32)] * 3
+        for l in range(LEVELS):
+            held = put_edges(held, l, [src[f, level + l, pl.ds(row, CHUNK), :] for f in range(FIELDS)])
+        return held
+
+    def post_edges(posted, i, held):
+        posted[0, i, 0] = jnp.where(low, pltpu.roll(held[1], WIDTH - 4, 1), held[0])
+        posted[0, i, 1] = held[2]
+        posted[1, i, 0] = jnp.where(low, held[0], pltpu.roll(held[1], 4, 1))
+        posted[1, i, 1] = held[2]
+
+    def pole_rows(sec, src, level, row):
+        mirror = lax.rem(11 - sub, 8)
+
+        @pl.loop(0, LEVELS)
+        def _(l):
+            for f in range(FIELDS):
+                value = jnp.take_along_axis(src[f, level + l, pl.ds(row, CHUNK), :], mirror, axis=0)
+                pole_out[sec, f, l] = (-value if flip[f] < 0 else value)[:4]
+
     load_kap.wait()
     kap = jnp.full((LEVELS, WIDTH), kap_s[0], jnp.float32)
     for l in range(1, LEVELS):
@@ -135,34 +171,6 @@
     @pl.when(stays)
     def _():
         kap_in[...] = kap
-
-    def put_edges(held, l, tiles):
-        held = list(held)
-        for f in range(FIELDS):
-            at = 8 * (f % 2) + l
-            held[f // 2] = jnp.where(group == at, pltpu.roll(tiles[f], (8 * at + 4) % WIDTH, 1), held[f // 2])
-        return held
-
-    def packed(src, level, row):
-        held = [jnp.zeros((CHUNK, WIDTH), jnp.float32)] * 3
-        for l in range(LEVELS):
-            held = put_edges(held, l, [src[f, level + l, pl.ds(row, CHUNK), :] for f in range(FIELDS)])
-        return held
-
-    def post_edges(sec, i, held):
-        edge_out[sec, 0, i, 0] = jnp.where(low, pltpu.roll(held[1], WIDTH - 4, 1), held[0])
-        edge_out[sec, 0, i, 1] = held[2]
-        edge_out[sec, 1, i, 0] = jnp.where(low, held[0], pltpu.roll(held[1], 4, 1))
-        edge_out[sec, 1, i, 1] = held[2]
-
-    def pole_rows(sec, src, level, row):
-        mirror = lax.rem(11 - sub, 8)
-
-        @pl.loop(0, LEVELS)
-        def _(l):
-            for f in range(FIELDS):
-                value = jnp.take_along_axis(src[f, level + l, pl.ds(row, CHUNK), :], mirror, axis=0)
-                pole_out[sec, f, l] = (-value if flip[f] < 0 else value)[:4]
 
     pl.semaphore_wait(
         barrier, 3 + swapped.astype(jnp.int32) + below.astype(jnp.int32) + above.astype(jnp.int32)
@@ -219,16 +227,34 @@
         def _():
             down.wait_recv()
 
+    def each_edge(sec, i, act):
+        to_left, to_right = edges(sec, i)
+        if sec == 1:
+            act(to_left)
+            act(to_right)
+        else:
+
+            @pl.when(stays | (side_of_pair == 0))
+            def _():
+                act(to_left)
+
+            @pl.when(stays | (side_of_pair == 1))
+            def _():
+                act(to_right)
+
+    home_edges = [
+        remote(home_out.at[1 - home_side, i], edge_in.at[0, home_side, i], home_send.at[i],
+               edge_recv.at[0, home_side, i], sibling)
+        for i in range(CHUNKS)
+    ]
+
     def send_edges(sec, i, src):
         if sec == 0:
             held = packed(src, 4, 8 + CHUNK * i)
-            for n in range(3):
-                edge_own[0, i, n] = held[n]
         else:
-            held = [edge_own[1, i, n] for n in range(3)]
-        post_edges(sec, i, held)
-        for c in edges(sec, i):
-            c.start()
+            held = [edge_own[i, n] for n in range(3)]
+        post_edges(edge_out.at[sec], i, held)
+        each_edge(sec, i, lambda c: c.start())
         if i == 0:
             pole_rows(sec, src, 4, 8)
             poles[sec].start()
@@ -243,10 +269,33 @@
     def _():
         for i in range(CHUNKS):
             send_levels(0, i, state, 0, False)
+
+    @pl.when(stays)
+    def _():
         for i in range(CHUNKS):
             keep[i].wait()
             send_edges(0, i, a)
 
+    @pl.when(swapped)
+    def _():
+        load_home.wait()
+
+        @pl.loop(0, CHUNKS)
+        def _(i):
+            post_edges(home_out, i, packed(home, 0, pl.multiple_of(CHUNK * i, CHUNK)))
+
+        for c in home_edges:
+            c.start()
+
+    edge_own[...] = jnp.zeros_like(edge_own)
+    tap = lax.broadcasted_iota(jnp.int32, (WIDTH, WIDTH), 0) - lax.broadcasted_iota(jnp.int32, (WIDTH, WIDTH), 1)
+    for n, (weights, sign) in enumerate(((first_taps, -1.0), (second_taps, 1.0))):
+        matrix = jnp.zeros((WIDTH, WIDTH), jnp.float32)
+        for k in range(1, 5):
+            matrix = jnp.where(tap == k, weights[k - 1], jnp.where(tap == -k, sign * weights[k - 1], matrix))
+        for part in range(3):
+            taps[n, pl.ds(WIDTH * part, WIDTH), :] = matrix.astype(jnp.bfloat16)
+
     spacing = 2.0 * math.pi / (WIDTH * lons)
 
     first_ratio = [c / first_coeffs[0] for c in first_coeffs]
@@ -256,7 +305,10 @@
     def weighed(terms, ratios):
         return terms[0] + ratios[1] * terms[1] + ratios[2] * terms[2] + ratios[3] * terms[3]
 
-    def seam(sec, i, own):
+    def summed(terms, weights):
+        return weights[0] * terms[0] + weights[1] * terms[1] + weights[2] * terms[2] + weights[3] * terms[3]
+
+    def seam(sec, i):
         left = [edge_in[sec, 0, i, n] for n in range(2)]
         right = [edge_in[sec, 1, i, n] for n in range(2)]
         beyond = (
@@ -266,44 +318,40 @@
         )
         found = []
         for n in range(3):
-            lack = beyond[n] - own[n]
+            lack = beyond[n]
             on_right = jnp.where(low, 0.0, lack)
             on_left = jnp.where(low, lack, 0.0)
             ahead = [pltpu.roll(on_right, WIDTH - k, 1) for k in range(1, 5)]
             behind = [pltpu.roll(on_left, k, 1) for k in range(1, 5)]
-            d = jnp.where(low, weighed(ahead, first_ratio), -weighed(behind, first_ratio))
+            d = jnp.where(low, summed(ahead, first_taps), -summed(behind, first_taps))
             if n == 2:
-                e = jnp.where(low, weighed(ahead, second_ratio), weighed(behind, second_ratio))
+                e = jnp.where(low, summed(ahead, second_taps), summed(behind, second_taps))
                 d = jnp.where(lane < 64, d, pltpu.roll(e, 64, 1))
             found.append(d)
         return found
 
-    def turned(q, m, d, ratios, sign):
-        even = ratios[2] * q + (0.5 * (ratios[1] + ratios[3])) * m
-        odd = (0.5 * (ratios[3] - ratios[1])) * d
-        ahead, behind = pltpu.roll(even + odd, WIDTH - 3, 1), pltpu.roll(even - odd, 3, 1)
-        return d + (ahead - behind) if sign < 0 else m + (ahead + behind)
-
-    def along_lon(src, i, extra):
-        def seam_of(n, at):
-            return jnp.where(across_seam, pltpu.roll(extra[n], WIDTH - 4 - 8 * at, 1), 0.0)
-
-        @pl.loop(0, LEVELS, unroll=UNROLL_LON)
-        def _(l):
-            for f in range(FIELDS):
-                q = src[f, l + 4, ext_rows(i), :]
-                ahead, behind = pltpu.roll(q, WIDTH - 1, 1), pltpu.roll(q, 1, 1)
-                m, d = ahead + behind, ahead - behind
-                along[f, l] = turned(q, m, d, first_ratio, -1) + seam_of(f // 2, 8 * (f % 2) + l)
-                if f == 4:
-                    along[5, l] = turned(q, m, d, second_ratio, 1) + seam_of(2, 8 + l)
-
-    def tendency(src, i, l, consts):
+    def along_lon(src, i):
+        q = src[:, own, ext_rows(i), :].reshape(FIELDS * LEVELS * CHUNK, WIDTH)
+        high = q.astype(jnp.bfloat16)
+        rest = q - high.astype(jnp.float32)
+        middle = rest.astype(jnp.bfloat16)
+        last = (rest - middle.astype(jnp.float32)).astype(jnp.bfloat16)
+        parts = jnp.concatenate([high, middle, last], axis=1)
+        slope = jnp.dot(parts, taps[0], preferred_element_type=jnp.float32)
+        along[:FIELDS] = slope.reshape(FIELDS, LEVELS, CHUNK, WIDTH)
+        second = jnp.dot(parts[4 * LEVELS * CHUNK :], taps[1], preferred_element_type=jnp.float32)
+        along[FIELDS] = second.reshape(LEVELS, CHUNK, WIDTH)
+
+    def tendency(src, i, l, extra, consts):
         stretch, turn, stretch2, centre = consts
         row = 8 + CHUNK * i
         cells = [src[f, l + 4, ext_rows(i), :] for f in range(FIELDS)]
         _, u_lon, u_row, u_lev, temper = cells
-        by_lon = [along[f, l] for f in range(FIELDS)]
+
+        def seam_of(n, at):
+            return jnp.where(across_seam, pltpu.roll(extra[n], WIDTH - 4 - 8 * at, 1), 0.0)
+
+        by_lon = [along[f, l] + seam_of(f // 2, 8 * (f % 2) + l) for f in range(FIELDS)]
         by_rows, by_level = [], []
         for f in range(FIELDS):
             row_d, lev_d, row_s, lev_s = [], [], [], []
@@ -321,7 +369,7 @@
             by_level.append(weighed(lev_d, first_ratio))
             if f == 4:
                 laplace = (
-                    stretch2 * along[5, l]
+                    stretch2 * (along[FIELDS, l] + seam_of(2, 8 + l))
                     + weighed(row_s, second_ratio)
                     + (radial_ratio * radial_ratio) * weighed(lev_s, second_ratio)
                     + centre * temper
@@ -342,35 +390,37 @@
         thetas = [(CHUNK * i + r + 0.5) * spacing for r in range(CHUNK)]
         metric = [1.0 / math.sin(t) for t in thetas]
         return (
-            by_row([step * m for m in metric], sub),
+            by_row([time_step / 840 * m for m in metric], sub),
             by_row([time_step * math.cos(t) * m for t, m in zip(thetas, metric)], sub),
-            by_row([m * m for m in metric], sub),
+            by_row([m * m / second_taps[0] for m in metric], sub),
             by_row([second_coeffs[0] / second_coeffs[1] * (m * m + 1 + radial_ratio**2) for m in metric], sub),
         )
 
     def first_section(i):
         consts = geometry(i)
-        along_lon(a, i, seam(0, i, [edge_own[0, i, n] for n in range(3)]))
+        extra = seam(0, i)
+        along_lon(a, i)
 
         @pl.loop(0, LEVELS, unroll=UNROLL)
         def _(l):
-            cells, rate = tendency(a, i, l, consts)
+            cells, rate = tendency(a, i, l, extra, consts)
             new = []
             for f in range(FIELDS):
                 first[f, l, rows_of(i), :] = rate[f]
                 new.append(cells[f] - rate[f])
                 b[f, l + 4, ext_rows(i), :] = new[f]
-            held = put_edges([edge_own[1, i, n] for n in range(3)], l, new)
+            held = put_edges([edge_own[i, n] for n in range(3)], l, new)
             for n in range(3):
-                edge_own[1, i, n] = held[n]
+                edge_own[i, n] = held[n]
 
     def second_section(i):
         consts = geometry(i)
-        along_lon(b, i, seam(1, i, [edge_own[1, i, n] for n in range(3)]))
+        extra = seam(1, i)
+        along_lon(b, i)
 
         @pl.loop(0, LEVELS, unroll=UNROLL)
         def _(l):
-            _, rate = tendency(b, i, l, consts)
+            _, rate = tendency(b, i, l, extra, consts)
             for f in range(FIELDS):
                 total[f, l, rows_of(i), :] = -0.5 * (first[f, l, rows_of(i), :] + rate[f])
 
@@ -391,7 +441,16 @@
         for i in range(CHUNKS)
     ]
 
-    for t in range(CHUNKS + 1 + LAG):
+    def finish(i, copies):
+        if i == 0:
+            take_pole(1, b)
+        await_levels(1, i)
+        for c in edges(1, i):
+            c.wait_recv()
+        second_section(i)
+        copies[i].start()
+
+    for t in range(CHUNKS + 1 + max(LAG, LAG_STAYS)):
         if t < CHUNKS:
 
             @pl.when(swapped)
@@ -438,29 +497,23 @@
                 move[t + AHEAD].start()
                 if t + AHEAD == CHUNKS - 1:
                     move_rows.start()
-        i = t - 1 - LAG
-        if 0 <= i < CHUNKS:
-            if i == 0:
-                take_pole(1, b)
-            await_levels(1, i)
-            for c in edges(1, i):
-                c.wait_recv()
-            second_section(i)
+        if 0 <= t - 1 - LAG < CHUNKS:
 
             @pl.when(swapped)
             def _():
-                give[i].start()
+                finish(t - 1 - LAG, give)
+
+        if 0 <= t - 1 - LAG_STAYS < CHUNKS:
 
             @pl.when(stays)
             def _():
-                put[i].start()
+                finish(t - 1 - LAG_STAYS, put)
 
     for c in poles:
         c.wait_send()
     for i in range(CHUNKS):
         for sec in range(2):
-            for c in edges(sec, i):
-                c.wait_send()
+            each_edge(sec, i, lambda c: c.wait_send())
             down, up = halo(sec, i, a if sec == 0 else b, 4, True)
 
             @pl.when(below)
@@ -478,7 +531,7 @@
 
     @pl.when(swapped)
     def _():
-        for c in (*move, move_rows, move_kap):
+        for c in (*move, *home_edges, move_rows, move_kap):
             c.wait_send()
         for c in give:
             c.wait()
@@ -493,7 +546,7 @@
         block = (FIELDS, LEVELS, ROWS, WIDTH)
         wide = (FIELDS, LEVELS + 8, ROWS + 16, WIDTH)
         edges = (2, 2, CHUNKS, 2, CHUNK, WIDTH)
-        own_edges = (2, CHUNKS, 3, CHUNK, WIDTH)
+        own_edges = (CHUNKS, 3, CHUNK, WIDTH)
         pole = (2, FIELDS, LEVELS, 4, WIDTH)
         return pl.pallas_call(
             functools.partial(kernel, lons, rads),
@@ -505,18 +558,20 @@
             ],
             out_specs=pl.BlockSpec(memory_space=pl.ANY),
             scratch_shapes=[
+                vmem(block, f32), vmem((2, CHUNKS, 2, CHUNK, WIDTH), f32),
                 vmem(wide, f32), vmem(wide, f32), vmem(block, f32), vmem(block, f32),
                 vmem((FIELDS + 1, LEVELS, CHUNK, WIDTH), f32),
                 vmem(own_edges, f32), vmem(edges, f32), vmem(edges, f32), vmem(pole, f32), vmem(pole, f32),
-                vmem((FIELDS, LEVELS, 4, WIDTH), f32), vmem((LEVELS, WIDTH), f32), vmem((LEVELS, WIDTH), f32), pltpu.SMEM((LEVELS,), f32),
-                dma, dma((CHUNKS,)), dma((CHUNKS,)), dma((2, 2, CHUNKS)), dma((2, 2, CHUNKS)),
+                vmem((FIELDS, LEVELS, 4, WIDTH), f32), vmem((LEVELS, WIDTH), f32), vmem((LEVELS, WIDTH), f32),
+                vmem((2, 3 * WIDTH, WIDTH), jnp.bfloat16), pltpu.SMEM((LEVELS,), f32),
+                dma, dma((CHUNKS,)), dma, dma((CHUNKS,)), dma((CHUNKS,)), dma((2, 2, CHUNKS)), dma((2, 2, CHUNKS)),
                 dma((2, 2, CHUNKS)), dma((2, 2, CHUNKS)),
                 dma((2,)), dma((2,)), dma, dma, dma, dma, dma((CHUNKS,)), dma((CHUNKS,)),
             ],
             compiler_params=pltpu.CompilerParams(
-                collective_id=0, has_side_effects=True, vmem_limit_bytes=66_000_000
+                collective_id=0, has_side_effects=True, vmem_limit_bytes=48_000_000
             ),
-        )(state, outer_rows, kappa)
+        )(*(pltpu.with_memory_space_constraint(x, pltpu.HBM) for x in (state, outer_rows, kappa)))
 
     placed = (P(None, "rad", None, "lon"), P(None, "rad", None, "lon"), P("rad"))
     return jax.shard_map(

time: 38.1 us -> 35.4 us (0.929)
  Pallas kernels: 35.8 us -> 34.1 us
  local copies, waits for them, and re-layouts: 2.24 us -> 0.95 us
    pallas_call x1, Pallas kernels: 35.8 us -> 34.1 us  [on_device(): pl.pallas_call(functools.partial(kernel, lons, rads), out_shape=jax.Shape...]
    unnamed x1, local copies, waits for them, and re-layouts: 2.24 us -> 0.95 us
where the time goes in v3:
time: 35.4 us; the launch traced here: 35.1 us
  Pallas kernels  34.1 us (96%)
  local copies, waits for them, and re-layouts  0.95 us (3%)
    pallas_call x1, Pallas kernels, on_device(): pl.pallas_call(functools.partial(kernel, lons, rads), out_shape=jax.Shape...  34.1 us
    unnamed x1, local copies, waits for them, and re-layouts  0.95 us

profile of v3, /device:TPU:98, one launch (start us, length us, event | category | flops | bytes accessed | tf_op | source)
XLA Modules:
  0.0 35.1 jit_solution(14787414818928196471)
XLA Ops:
  0.0 34.1 %shard_map.37 = f32[5,8,48,128]{3,2,1,0:T(8,128)S(1)} custom-call(f32[5,8,48,128]{3,2,1,0:T(8,128)} %state.1, f32[5,8,4,128]{3,2,1,0:T(4,128)} %outer.1, f32[8]{0:T(128)} %kappa.1), custom_call_target="tpu_custom_call" | custom-call | tf_op jit(solution)/shard_map/pallas_call | solution.py:551
  34.2 0.9 %copy.5 = f32[5,8,48,128]{3,2,1,0:T(8,128)} copy(f32[5,8,48,128]{3,2,1,0:T(8,128)S(1)} %shard_map.37) | data formatting | bytes 1966080

commit v4 on v3

--- a/solution.py
+++ b/solution.py
@@ -21,7 +21,7 @@
 CHUNKS = ROWS // CHUNK
 LAG, LAG_STAYS = 3, 5
 AHEAD = 4
-UNROLL = 2
+UNROLL = 4
 MESH = pl.DeviceIdType.MESH
 flip = (1.0, -1.0, -1.0, 1.0, 1.0)
 
@@ -40,7 +40,7 @@
 
 def kernel(
     lons, rads, state, outer, kappa, out,
-    home, home_out, a, b, first, total, along, edge_own, edge_out, edge_in, pole_out, pole_in, rows_in, kap_out, kap_in, taps, kap_s,
+    home, home_out, a, b, first, total, along, south_d, up_d, rest, edge_own, edge_out, edge_in, pole_out, pole_in, rows_in, kap_out, kap_in, taps, kap_s,
     home_sem, home_send, kap_sem, in_recv, in_send, lev_recv, lev_send, edge_recv, edge_send,
     pole_recv, pole_send, rows_recv, rows_send, kap_recv, kap_send, out_recv, out_send,
 ):
@@ -160,17 +160,6 @@
             for f in range(FIELDS):
                 value = jnp.take_along_axis(src[f, level + l, pl.ds(row, CHUNK), :], mirror, axis=0)
                 pole_out[sec, f, l] = (-value if flip[f] < 0 else value)[:4]
-
-    load_kap.wait()
-    kap = jnp.full((LEVELS, WIDTH), kap_s[0], jnp.float32)
-    for l in range(1, LEVELS):
-        kap = jnp.where(sub == l, kap_s[l], kap)
-    kap = kap * (time_step * second_coeffs[1])
-    kap_out[...] = kap
-
-    @pl.when(stays)
-    def _():
-        kap_in[...] = kap
 
     pl.semaphore_wait(
         barrier, 3 + swapped.astype(jnp.int32) + below.astype(jnp.int32) + above.astype(jnp.int32)
@@ -261,8 +250,24 @@
 
     @pl.when(swapped)
     def _():
+        for c in move[:2]:
+            c.start()
+
+    load_kap.wait()
+    kap = jnp.full((LEVELS, WIDTH), kap_s[0], jnp.float32)
+    for l in range(1, LEVELS):
+        kap = jnp.where(sub == l, kap_s[l], kap)
+    kap = kap * (time_step * second_coeffs[1])
+    kap_out[...] = kap
+
+    @pl.when(stays)
+    def _():
+        kap_in[...] = kap
+
+    @pl.when(swapped)
+    def _():
         move_kap.start()
-        for c in move[:AHEAD]:
+        for c in move[2:AHEAD]:
             c.start()
 
     @pl.when(stays)
@@ -342,9 +347,30 @@
         second = jnp.dot(parts[4 * LEVELS * CHUNK :], taps[1], preferred_element_type=jnp.float32)
         along[FIELDS] = second.reshape(LEVELS, CHUNK, WIDTH)
 
+    def across_rows_and_levels(src, i):
+        row = 8 + CHUNK * i
+        for f in range(FIELDS):
+            column = [src[f, n, ext_rows(i), :] for n in range(LEVELS + 8)]
+            for l in range(LEVELS):
+                row_d, lev_d, row_s, lev_s = [], [], [], []
+                for k in range(1, 5):
+                    south = src[f, l + 4, pl.ds(row + k, CHUNK), :]
+                    north = src[f, l + 4, pl.ds(row - k, CHUNK), :]
+                    over, under = column[l + 4 + k], column[l + 4 - k]
+                    row_d.append(south - north)
+                    lev_d.append(over - under)
+                    if f == 4:
+                        row_s.append(south + north)
+                        lev_s.append(over + under)
+                south_d[f, l] = weighed(row_d, first_ratio)
+                up_d[f, l] = weighed(lev_d, first_ratio)
+                if f == 4:
+                    rest[l] = weighed(row_s, second_ratio) + (radial_ratio * radial_ratio) * weighed(
+                        lev_s, second_ratio
+                    )
+
     def tendency(src, i, l, extra, consts):
         stretch, turn, stretch2, centre = consts
-        row = 8 + CHUNK * i
         cells = [src[f, l + 4, ext_rows(i), :] for f in range(FIELDS)]
         _, u_lon, u_row, u_lev, temper = cells
 
@@ -352,28 +378,9 @@
             return jnp.where(across_seam, pltpu.roll(extra[n], WIDTH - 4 - 8 * at, 1), 0.0)
 
         by_lon = [along[f, l] + seam_of(f // 2, 8 * (f % 2) + l) for f in range(FIELDS)]
-        by_rows, by_level = [], []
-        for f in range(FIELDS):
-            row_d, lev_d, row_s, lev_s = [], [], [], []
-            for k in range(1, 5):
-                south = src[f, l + 4, pl.ds(row + k, CHUNK), :]
-                north = src[f, l + 4, pl.ds(row - k, CHUNK), :]
-                over = src[f, l + 4 + k, ext_rows(i), :]
-                under = src[f, l + 4 - k, ext_rows(i), :]
-                row_d.append(south - north)
-                lev_d.append(over - under)
-                if f == 4:
-                    row_s.append(south + north)
-                    lev_s.append(over + under)
-            by_rows.append(weighed(row_d, first_ratio))
-            by_level.append(weighed(lev_d, first_ratio))
-            if f == 4:
-                laplace = (
-                    stretch2 * (along[FIELDS, l] + seam_of(2, 8 + l))
-                    + weighed(row_s, second_ratio)
-                    + (radial_ratio * radial_ratio) * weighed(lev_s, second_ratio)
-                    + centre * temper
-                )
+        by_rows = [south_d[f, l] for f in range(FIELDS)]
+        by_level = [up_d[f, l] for f in range(FIELDS)]
+        laplace = stretch2 * (along[FIELDS, l] + seam_of(2, 8 + l)) + rest[l] + centre * temper
         to_lon, to_row, to_lev = stretch * u_lon, step * u_row, (radial_ratio * step) * u_lev
         carried = [to_lon * by_lon[f] + to_row * by_rows[f] + to_lev * by_level[f] for f in range(FIELDS)]
         spread = stretch * by_lon[1] + step * (by_rows[2] + radial_ratio * by_level[3]) + turn * u_row
@@ -400,6 +407,7 @@
         consts = geometry(i)
         extra = seam(0, i)
         along_lon(a, i)
+        across_rows_and_levels(a, i)
 
         @pl.loop(0, LEVELS, unroll=UNROLL)
         def _(l):
@@ -417,6 +425,7 @@
         consts = geometry(i)
         extra = seam(1, i)
         along_lon(b, i)
+        across_rows_and_levels(b, i)
 
         @pl.loop(0, LEVELS, unroll=UNROLL)
         def _(l):
@@ -560,7 +569,8 @@
             scratch_shapes=[
                 vmem(block, f32), vmem((2, CHUNKS, 2, CHUNK, WIDTH), f32),
                 vmem(wide, f32), vmem(wide, f32), vmem(block, f32), vmem(block, f32),
-                vmem((FIELDS + 1, LEVELS, CHUNK, WIDTH), f32),
+                vmem((FIELDS + 1, LEVELS, CHUNK, WIDTH), f32), vmem((FIELDS, LEVELS, CHUNK, WIDTH), f32),
+                vmem((FIELDS, LEVELS, CHUNK, WIDTH), f32), vmem((LEVELS, CHUNK, WIDTH), f32),
                 vmem(own_edges, f32), vmem(edges, f32), vmem(edges, f32), vmem(pole, f32), vmem(pole, f32),
                 vmem((FIELDS, LEVELS, 4, WIDTH), f32), vmem((LEVELS, WIDTH), f32), vmem((LEVELS, WIDTH), f32),
                 vmem((2, 3 * WIDTH, WIDTH), jnp.bfloat16), pltpu.SMEM((LEVELS,), f32),

time: 35.4 us -> 35.1 us (level)
  no operation moved by 1% of the time
where the time goes in v4:
time: 35.1 us; the launch traced here: 34.9 us
  Pallas kernels  33.9 us (97%)
  local copies, waits for them, and re-layouts  0.95 us (3%)
    pallas_call x1, Pallas kernels, on_device(): pl.pallas_call(functools.partial(kernel, lons, rads), out_shape=jax.Shape...  33.9 us
    unnamed x1, local copies, waits for them, and re-layouts  0.95 us

profile of v4, /device:TPU:98, one launch (start us, length us, event | category | flops | bytes accessed | tf_op | source)
XLA Modules:
  0.0 34.9 jit_solution(1509132528867358908)
XLA Ops:
  0.0 33.9 %shard_map.37 = f32[5,8,48,128]{3,2,1,0:T(8,128)S(1)} custom-call(f32[5,8,48,128]{3,2,1,0:T(8,128)} %state.1, f32[5,8,4,128]{3,2,1,0:T(4,128)} %outer.1, f32[8]{0:T(128)} %kappa.1), custom_call_target="tpu_custom_call" | custom-call | tf_op jit(solution)/shard_map/pallas_call | solution.py:560
  33.9 0.9 %copy.5 = f32[5,8,48,128]{3,2,1,0:T(8,128)} copy(f32[5,8,48,128]{3,2,1,0:T(8,128)S(1)} %shard_map.37) | data formatting | bytes 1966080

commit v5 on v4

--- a/solution.py
+++ b/solution.py
@@ -40,7 +40,7 @@
 
 def kernel(
     lons, rads, state, outer, kappa, out,
-    home, home_out, a, b, first, total, along, south_d, up_d, rest, edge_own, edge_out, edge_in, pole_out, pole_in, rows_in, kap_out, kap_in, taps, kap_s,
+    home, home_out, a, b, first, total, along, along2, south_d, south2, up_d, rest, rest2, edge_own, edge_out, edge_in, pole_out, pole_in, rows_in, kap_out, kap_in, taps, kap_s,
     home_sem, home_send, kap_sem, in_recv, in_send, lev_recv, lev_send, edge_recv, edge_send,
     pole_recv, pole_send, rows_recv, rows_send, kap_recv, kap_send, out_recv, out_send,
 ):
@@ -335,7 +335,7 @@
             found.append(d)
         return found
 
-    def along_lon(src, i):
+    def along_lon(src, i, to):
         q = src[:, own, ext_rows(i), :].reshape(FIELDS * LEVELS * CHUNK, WIDTH)
         high = q.astype(jnp.bfloat16)
         rest = q - high.astype(jnp.float32)
@@ -343,33 +343,31 @@
         last = (rest - middle.astype(jnp.float32)).astype(jnp.bfloat16)
         parts = jnp.concatenate([high, middle, last], axis=1)
         slope = jnp.dot(parts, taps[0], preferred_element_type=jnp.float32)
-        along[:FIELDS] = slope.reshape(FIELDS, LEVELS, CHUNK, WIDTH)
+        to[:FIELDS] = slope.reshape(FIELDS, LEVELS, CHUNK, WIDTH)
         second = jnp.dot(parts[4 * LEVELS * CHUNK :], taps[1], preferred_element_type=jnp.float32)
-        along[FIELDS] = second.reshape(LEVELS, CHUNK, WIDTH)
-
-    def across_rows_and_levels(src, i):
+        to[FIELDS] = second.reshape(LEVELS, CHUNK, WIDTH)
+
+    def row_slopes(src, i, to, second):
         row = 8 + CHUNK * i
+        for f in range(FIELDS):
+            for l in range(LEVELS):
+                south = [src[f, l + 4, pl.ds(row + k, CHUNK), :] for k in range(1, 5)]
+                north = [src[f, l + 4, pl.ds(row - k, CHUNK), :] for k in range(1, 5)]
+                to[f, l] = weighed([x - y for x, y in zip(south, north)], first_ratio)
+                if f == 4:
+                    second[l] = weighed([x + y for x, y in zip(south, north)], second_ratio)
+
+    def level_slopes(src, i, second):
         for f in range(FIELDS):
             column = [src[f, n, ext_rows(i), :] for n in range(LEVELS + 8)]
             for l in range(LEVELS):
-                row_d, lev_d, row_s, lev_s = [], [], [], []
-                for k in range(1, 5):
-                    south = src[f, l + 4, pl.ds(row + k, CHUNK), :]
-                    north = src[f, l + 4, pl.ds(row - k, CHUNK), :]
-                    over, under = column[l + 4 + k], column[l + 4 - k]
-                    row_d.append(south - north)
-                    lev_d.append(over - under)
-                    if f == 4:
-                        row_s.append(south + north)
-                        lev_s.append(over + under)
-                south_d[f, l] = weighed(row_d, first_ratio)
-                up_d[f, l] = weighed(lev_d, first_ratio)
+                over, under = column[l + 5 : l + 9], column[l : l + 4][::-1]
+                up_d[f, l] = weighed([x - y for x, y in zip(over, under)], first_ratio)
                 if f == 4:
-                    rest[l] = weighed(row_s, second_ratio) + (radial_ratio * radial_ratio) * weighed(
-                        lev_s, second_ratio
-                    )
-
-    def tendency(src, i, l, extra, consts):
+                    lev_s = weighed([x + y for x, y in zip(over, under)], second_ratio)
+                    rest[l] = second[l] + (radial_ratio * radial_ratio) * lev_s
+
+    def tendency(src, i, l, extra, consts, along, south_d):
         stretch, turn, stretch2, centre = consts
         cells = [src[f, l + 4, ext_rows(i), :] for f in range(FIELDS)]
         _, u_lon, u_row, u_lev, temper = cells
@@ -406,12 +404,13 @@
     def first_section(i):
         consts = geometry(i)
         extra = seam(0, i)
-        along_lon(a, i)
-        across_rows_and_levels(a, i)
+        along_lon(a, i, along)
+        row_slopes(a, i, south_d, rest)
+        level_slopes(a, i, rest)
 
         @pl.loop(0, LEVELS, unroll=UNROLL)
         def _(l):
-            cells, rate = tendency(a, i, l, extra, consts)
+            cells, rate = tendency(a, i, l, extra, consts, along, south_d)
             new = []
             for f in range(FIELDS):
                 first[f, l, rows_of(i), :] = rate[f]
@@ -424,12 +423,11 @@
     def second_section(i):
         consts = geometry(i)
         extra = seam(1, i)
-        along_lon(b, i)
-        across_rows_and_levels(b, i)
+        level_slopes(b, i, rest2.at[i])
 
         @pl.loop(0, LEVELS, unroll=UNROLL)
         def _(l):
-            _, rate = tendency(b, i, l, extra, consts)
+            _, rate = tendency(b, i, l, extra, consts, along2.at[i], south2.at[i])
             for f in range(FIELDS):
                 total[f, l, rows_of(i), :] = -0.5 * (first[f, l, rows_of(i), :] + rate[f])
 
@@ -453,6 +451,7 @@
     def finish(i, copies):
         if i == 0:
             take_pole(1, b)
+            row_slopes(b, 0, south2.at[0], rest2.at[0])
         await_levels(1, i)
         for c in edges(1, i):
             c.wait_recv()
@@ -518,6 +517,12 @@
             def _():
                 finish(t - 1 - LAG_STAYS, put)
 
+        if 0 <= i < CHUNKS:
+            along_lon(b, i, along2.at[i])
+            for n in range(i - 1, i if i < CHUNKS - 1 else i + 1):
+                if n > 0:
+                    row_slopes(b, n, south2.at[n], rest2.at[n])
+
     for c in poles:
         c.wait_send()
     for i in range(CHUNKS):
@@ -556,6 +561,7 @@
         wide = (FIELDS, LEVELS + 8, ROWS + 16, WIDTH)
         edges = (2, 2, CHUNKS, 2, CHUNK, WIDTH)
         own_edges = (CHUNKS, 3, CHUNK, WIDTH)
+        tiles = (LEVELS, CHUNK, WIDTH)
         pole = (2, FIELDS, LEVELS, 4, WIDTH)
         return pl.pallas_call(
             functools.partial(kernel, lons, rads),
@@ -569,8 +575,9 @@
             scratch_shapes=[
                 vmem(block, f32), vmem((2, CHUNKS, 2, CHUNK, WIDTH), f32),
                 vmem(wide, f32), vmem(wide, f32), vmem(block, f32), vmem(block, f32),
-                vmem((FIELDS + 1, LEVELS, CHUNK, WIDTH), f32), vmem((FIELDS, LEVELS, CHUNK, WIDTH), f32),
-                vmem((FIELDS, LEVELS, CHUNK, WIDTH), f32), vmem((LEVELS, CHUNK, WIDTH), f32),
+                vmem((FIELDS + 1, *tiles), f32), vmem((CHUNKS, FIELDS + 1, *tiles), f32),
+                vmem((FIELDS, *tiles), f32), vmem((CHUNKS, FIELDS, *tiles), f32),
+                vmem((FIELDS, *tiles), f32), vmem(tiles, f32), vmem((CHUNKS, *tiles), f32),
                 vmem(own_edges, f32), vmem(edges, f32), vmem(edges, f32), vmem(pole, f32), vmem(pole, f32),
                 vmem((FIELDS, LEVELS, 4, WIDTH), f32), vmem((LEVELS, WIDTH), f32), vmem((LEVELS, WIDTH), f32),
                 vmem((2, 3 * WIDTH, WIDTH), jnp.bfloat16), pltpu.SMEM((LEVELS,), f32),

time: 35.1 us -> 35.1 us (level)
  no operation moved by 1% of the time
where the time goes in v5:
time: 35.1 us; the launch traced here: 34.8 us
  Pallas kernels  33.8 us (96%)
  local copies, waits for them, and re-layouts  0.95 us (3%)
    pallas_call x1, Pallas kernels, on_device(): pl.pallas_call(functools.partial(kernel, lons, rads), out_shape=jax.Shape...  33.8 us
    unnamed x1, local copies, waits for them, and re-layouts  0.95 us

profile of v5, /device:TPU:98, one launch (start us, length us, event | category | flops | bytes accessed | tf_op | source)
XLA Modules:
  0.0 34.8 jit_solution(13204895745531033239)
XLA Ops:
  0.0 33.8 %shard_map.37 = f32[5,8,48,128]{3,2,1,0:T(8,128)S(1)} custom-call(f32[5,8,48,128]{3,2,1,0:T(8,128)} %state.1, f32[5,8,4,128]{3,2,1,0:T(4,128)} %outer.1, f32[8]{0:T(128)} %kappa.1), custom_call_target="tpu_custom_call" | custom-call | tf_op jit(solution)/shard_map/pallas_call | solution.py:566
  33.8 0.9 %copy.5 = f32[5,8,48,128]{3,2,1,0:T(8,128)} copy(f32[5,8,48,128]{3,2,1,0:T(8,128)S(1)} %shard_map.37) | data formatting | bytes 1966080

commit v6 on v5

--- a/solution.py
+++ b/solution.py
@@ -420,16 +420,20 @@
             for n in range(3):
                 edge_own[i, n] = held[n]
 
-    def second_section(i):
+    def second_section(i, copies):
         consts = geometry(i)
         extra = seam(1, i)
         level_slopes(b, i, rest2.at[i])
 
-        @pl.loop(0, LEVELS, unroll=UNROLL)
-        def _(l):
-            _, rate = tendency(b, i, l, extra, consts, along2.at[i], south2.at[i])
-            for f in range(FIELDS):
-                total[f, l, rows_of(i), :] = -0.5 * (first[f, l, rows_of(i), :] + rate[f])
+        for part in range(2):
+
+            @pl.loop(4 * part, 4 * part + 4, unroll=UNROLL)
+            def _(l):
+                _, rate = tendency(b, i, l, extra, consts, along2.at[i], south2.at[i])
+                for f in range(FIELDS):
+                    total[f, l, rows_of(i), :] = -0.5 * (first[f, l, rows_of(i), :] + rate[f])
+
+            copies[part].start()
 
     def take_pole(sec, dst):
         poles[sec].wait_recv()
@@ -439,12 +443,18 @@
             for f in range(FIELDS):
                 dst[f, l + 4, pl.ds(4, 4), :] = pole_in[sec, f, l]
 
+    def part_of(ref, i, part):
+        return ref.at[:, pl.ds(4 * part, 4), rows_of(i), :]
+
     give = [
-        remote(total.at[:, :, rows_of(i), :], out.at[:, :, rows_of(i), :], out_send.at[i], out_recv.at[i], partner)
+        [
+            remote(part_of(total, i, n), part_of(out, i, n), out_send.at[i, n], out_recv.at[i, n], partner)
+            for n in range(2)
+        ]
         for i in range(CHUNKS)
     ]
     put = [
-        pltpu.make_async_copy(total.at[:, :, rows_of(i), :], out.at[:, :, rows_of(i), :], out_send.at[i])
+        [pltpu.make_async_copy(part_of(total, i, n), part_of(out, i, n), out_send.at[i, n]) for n in range(2)]
         for i in range(CHUNKS)
     ]
 
@@ -455,8 +465,7 @@
         await_levels(1, i)
         for c in edges(1, i):
             c.wait_recv()
-        second_section(i)
-        copies[i].start()
+        second_section(i, copies[i])
 
     for t in range(CHUNKS + 1 + max(LAG, LAG_STAYS)):
         if t < CHUNKS:
@@ -540,15 +549,17 @@
 
     @pl.when(stays)
     def _():
-        for c in put:
-            c.wait()
+        for halves in put:
+            for c in halves:
+                c.wait()
 
     @pl.when(swapped)
     def _():
         for c in (*move, *home_edges, move_rows, move_kap):
             c.wait_send()
-        for c in give:
-            c.wait()
+        for halves in give:
+            for c in halves:
+                c.wait()
 
 
 def solution(mesh):
@@ -583,7 +594,7 @@
                 vmem((2, 3 * WIDTH, WIDTH), jnp.bfloat16), pltpu.SMEM((LEVELS,), f32),
                 dma, dma((CHUNKS,)), dma, dma((CHUNKS,)), dma((CHUNKS,)), dma((2, 2, CHUNKS)), dma((2, 2, CHUNKS)),
                 dma((2, 2, CHUNKS)), dma((2, 2, CHUNKS)),
-                dma((2,)), dma((2,)), dma, dma, dma, dma, dma((CHUNKS,)), dma((CHUNKS,)),
+                dma((2,)), dma((2,)), dma, dma, dma, dma, dma((CHUNKS, 2)), dma((CHUNKS, 2)),
             ],
             compiler_params=pltpu.CompilerParams(
                 collective_id=0, has_side_effects=True, vmem_limit_bytes=48_000_000

time: 35.1 us -> 35 us (level)
  no operation moved by 1% of the time
where the time goes in v6:
time: 35 us; the launch traced here: 34.6 us
  Pallas kernels  33.6 us (96%)
  local copies, waits for them, and re-layouts  0.95 us (3%)
    pallas_call x1, Pallas kernels, on_device(): pl.pallas_call(functools.partial(kernel, lons, rads), out_shape=jax.Shape...  33.6 us
    unnamed x1, local copies, waits for them, and re-layouts  0.95 us

profile of v6, /device:TPU:98, one launch (start us, length us, event | category | flops | bytes accessed | tf_op | source)
XLA Modules:
  0.0 34.6 jit_solution(3807381400330131570)
XLA Ops:
  0.0 33.6 %shard_map.37 = f32[5,8,48,128]{3,2,1,0:T(8,128)S(1)} custom-call(f32[5,8,48,128]{3,2,1,0:T(8,128)} %state.1, f32[5,8,4,128]{3,2,1,0:T(4,128)} %outer.1, f32[8]{0:T(128)} %kappa.1), custom_call_target="tpu_custom_call" | custom-call | tf_op jit(solution)/shard_map/pallas_call | solution.py:577
  33.6 0.9 %copy.5 = f32[5,8,48,128]{3,2,1,0:T(8,128)} copy(f32[5,8,48,128]{3,2,1,0:T(8,128)S(1)} %shard_map.37) | data formatting | bytes 1966080
